TPU v7x, 1024 devices: a whole 4x4x32 slice. The times are simulated.
1024 devices in a mesh: dp: 64 (over z, core), seq: 8 (over y_lo, x), mp: 2 (over y_hi).
Axes of the slice: x: 4, y: 4 (y_hi: 2, y_lo: 2; y = y_hi * 2 + y_lo), z: 32, core: 2. Of those that a mesh axis runs over, the one named last changes fastest.
Arguments:
- queries: bfloat16 [64, 1024, 768], P('dp', 'seq', 'mp'), may hold values from -60 to 60
- keys: bfloat16 [64, 1024, 768], P('dp', 'seq', 'mp'), may hold values from -8 to 8
- values: bfloat16 [64, 1024, 768], P('dp', 'seq', 'mp'), may hold values from -6 to 6
- proj_weight: bfloat16 [2, 384, 1536], P('mp', 'dp'), may hold values from -0.5 to 0.5
- gate_table: float32 [4, 1536], replicated, may hold values from -6 to 6
- timestep: int32 [64], P('dp'), may hold values from 0 to 3
- span_index: int32 [64], P('dp'), may hold values from 0 to 7
- cotangent: bfloat16 [64, 1024, 1536], P('dp', 'seq'), may hold values from -0.0625 to 0.0625
Outputs:
- output: bfloat16 [64, 1024, 1536], P('dp', ('seq', 'mp'))
- weight_grad: float32 [2, 4608, 128], P('mp', ('dp', 'seq'))
All inputs are finite; a program needn't handle non-finite values.
Results may differ from a plain program's by a relative error of at most 0.015.
Values may be sent and summed in bfloat16 or wider, within the bound.
No kernel may reach another device: no remote copies, remote signals or barrier semaphores. Data moves between devices by JAX's collectives and lax.ppermute only.
A program may use at most 32 MiB of HBM per device.

v0:
```python
import jax
import jax.numpy as jnp
from jax import lax
from jax.sharding import PartitionSpec as P

HEAD = 128


def local(queries, keys, values, proj_weight, gate_table, timestep, span_index, cotangent):
    tok_rows = queries.shape[1]
    width = queries.shape[2]
    heads_here = width // HEAD
    inv_root = HEAD ** (-0.5)
    seq_place = lax.axis_index("seq")
    all_keys, all_values = (
        lax.all_gather(keys[0], "seq", axis=0, tiled=True),
        lax.all_gather(values[0], "seq", axis=0, tiled=True),
    )
    key_count = all_keys.shape[0]
    query_heads = queries[0].reshape(tok_rows, heads_here, HEAD)
    key_heads = all_keys.reshape(key_count, heads_here, HEAD)
    value_heads = all_values.reshape(key_count, heads_here, HEAD)
    scores = (
        jnp.einsum("qhd,khd->hqk", query_heads, key_heads, preferred_element_type=jnp.float32)
        * inv_root
    )
    key_span = jnp.arange(key_count, dtype=jnp.int32) // tok_rows
    visible = key_span <= jnp.minimum(seq_place, span_index[0])
    scores = jnp.where(visible[None, None, :], scores, -jnp.inf)
    row_top = jnp.max(scores, axis=2, keepdims=True)
    weights = jnp.exp(scores - row_top)
    probs = (weights / jnp.sum(weights, axis=2, keepdims=True)).astype(jnp.bfloat16)
    attended = jnp.einsum("hqk,khd->qhd", probs, value_heads, preferred_element_type=jnp.float32)
    attended = attended.reshape(tok_rows, width).astype(jnp.bfloat16)
    weight_rows = lax.all_gather(proj_weight, "dp", axis=1, tiled=True)
    mixed = jnp.dot(attended, weight_rows[0], preferred_element_type=jnp.float32)
    shared = lax.psum_scatter(
        mixed.astype(jnp.bfloat16), "mp", scatter_dimension=0, tiled=True
    ).astype(jnp.float32)
    step_hit = jnp.arange(gate_table.shape[0], dtype=jnp.int32) == timestep[0]
    gate = jnp.sum(jnp.where(step_hit[:, None], gate_table, 0.0), axis=0)
    output = (gate[None, :] * shared).astype(jnp.bfloat16)[None]
    scaled = (gate[None, :] * cotangent[0].astype(jnp.float32)).astype(jnp.bfloat16)
    term = jnp.dot(attended.T, scaled, preferred_element_type=jnp.float32).reshape(-1, 128)
    rows_all = term.shape[0]
    dp_count = lax.axis_size("dp")
    seq_count = lax.axis_size("seq")
    block_rows = rows_all // (dp_count * seq_count)
    grid_view = term.reshape(dp_count, seq_count, block_rows, 128)
    local_sum = lax.psum_scatter(
        grid_view.transpose(1, 0, 2, 3)
        .reshape(lax.axis_size("seq") * (rows_all // seq_count), 128)
        .astype(jnp.bfloat16),
        "seq",
        scatter_dimension=0,
        tiled=True,
    ).astype(jnp.float32)
    piece = lax.psum_scatter(local_sum, "dp", scatter_dimension=0, tiled=True)
    return (output, piece[None])


def solution(mesh):
    return jax.shard_map(
        local,
        mesh=mesh,
        in_specs=(
            P("dp", "seq", "mp"),
            P("dp", "seq", "mp"),
            P("dp", "seq", "mp"),
            P("mp", "dp", None),
            P(),
            P("dp"),
            P("dp"),
            P("dp", "seq", None),
        ),
        out_specs=(P("dp", ("seq", "mp"), None), P("mp", ("dp", "seq"), None)),
        check_vma=False,
    )
```

profile of v0, /device:TPU:2, one launch (start us, length us, event | category | flops | bytes accessed | tf_op | source)
XLA Modules:
  0.0 355.1 jit_solution(2932694985730581416)
XLA Ops:
  8.0 0.0 copy-start.1
  8.0 0.0 all-gather.4.cloned.1.call-start
  8.1 1.4 copy.33
  9.4 0.0 all-gather.4.cloned.1.call-update
  9.5 0.0 reduce-scatter.5.cloned.1.call-start
  9.5 1.0 copy.29
  10.5 1.0 copy.28
  12.2 39.2 %all-gather.1 = bf16[1,1024,384]{2,1,0:T(8,128)(2,1)S(1)} all-gather(bf16[1,128,384]{2,1,0:T(8,128)(2,1)} %param.10), channel_id=3, replica_groups=mesh['dp'=64,'seq'=8,'mp'=2] {'seq'}, dimensions={1}, use_global_device_ids=true | all-gather | bytes 884736 | tf_op jit(solution)/shard_map/all_gather | solution.py:17
  51.4 0.3 copy.32
  52.4 0.0 copy-done.1
  52.4 0.1 select_reduce_fusion
  52.5 26.7 %all-gather = bf16[1,1024,384]{1,2,0:T(8,128)(2,1)S(1)} all-gather(bf16[1,128,384]{1,2,0:T(8,128)(2,1)S(1)} %copy.29), channel_id=2, replica_groups=mesh['dp'=64,'seq'=8,'mp'=2] {'seq'}, dimensions={1}, use_global_device_ids=true | all-gather | bytes 884736 | tf_op jit(solution)/shard_map/all_gather | solution.py:16
  79.2 0.8 fusion.16
  80.0 0.0 copy-start
  80.0 0.5 convolution_convert_fusion.2
  80.5 0.5 copy-done
  81.0 0.5 convolution_convert_fusion
  81.5 1.4 convert_element_type.58
  82.9 1.7 copy.34
  84.6 3.6 %convert_element_type.60 = bf16[4608,128]{1,0:T(8,128)(2,1)} reshape(bf16[8,64,9,128]{3,2,1,0:T(8,128)(2,1)} %copy.34) | data formatting | bytes 2359296 | tf_op jit(solution)/shard_map/convert_element_type | solution.py:53
  88.2 0.0 reduce-scatter.5.cloned.1.call-update
  88.2 0.0 reduce-scatter.3.cloned.1.call-start
  88.3 68.4 %all-gather.4.cloned.1.call-done = bf16[1,384,1536]{2,0,1:T(2,128)(2,1)} async-done(((bf16[1,6,1536]{2,0,1:T(2,128)(2,1)}), bf16[1,384,1536]{2,0,1:T(2,128)(2,1)}) %all-gather.4.cloned.1.call-update) | async-done | bytes 1179664 | tf_op jit(solution)/shard_map/all_gather | solution.py:35
  156.7 2.8 convolution_convert_fusion.1
  159.5 0.0 reduce-scatter.3.cloned.1.call-update
  159.5 1.3 dynamic-slice
  161.4 0.0 reduce-scatter.5.cloned.1.call-done
  161.5 183.9 %all-reduce.2 = f32[576,128]{1,0:T(8,128)S(1)} all-reduce(bf16[576,128]{1,0:T(8,128)(2,1)} %reduce-scatter.5.cloned.1.call-done), channel_id=6, replica_groups=mesh['dp'=64,'seq'=8,'mp'=2] {'dp'}, use_global_device_ids=true, to_apply=%region_5.6.clone | all-reduce | flops 73728 | bytes 442368
  345.4 0.6 copy.35
  346.0 0.0 reduce-scatter.3.cloned.1.call-done
  346.0 1.6 fusion.8
  (3 shorter events, 0.0 us)
Async XLA Ops:
  8.0 44.4 %copy-start.1 = (f32[4,1536]{1,0:T(4,128)S(1)}, f32[4,1536]{1,0:T(4,128)}, u32[]{:S(2)}) copy-start(f32[4,1536]{1,0:T(4,128)} %param.12) | copy-start | bytes 73732
  8.0 148.6 %all-gather.4.cloned.1.call-start = ((), (), s32[]{:S(2)}) async-start(), calls=%async_computation.2 | async-start | bytes 2396160 | tf_op jit(solution)/shard_map/all_gather | solution.py:35
  9.5 152.0 %reduce-scatter.5.cloned.1.call-start = ((), (), s32[]{:S(2)}) async-start(), calls=%async_computation.4 | async-start | bytes 1327104 | tf_op jit(solution)/shard_map/reduce_scatter | solution.py:50
  80.0 1.0 copy-start
  88.2 257.8 %reduce-scatter.3.cloned.1.call-start = ((), (), s32[]{:S(2)}) async-start(), calls=%async_computation.3 | async-start | bytes 589824 | tf_op jit(solution)/shard_map/reduce_scatter | solution.py:37
Sparse Core Ops, SparseCore 0:
  12.1 144.5 all-gather.3
Sparse Core Ops, SparseCore 1:
  88.3 54.3 reduce-scatter.4
  159.6 26.2 reduce-scatter.2
where the time goes:
time: 356 us; the launch traced here: 355 us
  blocking collectives  250 us (70%)
  waiting for transfers between devices  68.5 us (19%)
  between operations  17.5 us (5%)
  local copies, waits for them, and re-layouts  12.8 us (4%)
  matrix products  4.5 us (1%)
    unnamed x1, blocking collectives  184 us
    all_gather x1, waiting for transfers between devices, local(): weight_rows = lax.all_gather(proj_weight, 'dp', axis=1, tiled=True)  68.4 us
    all_gather x1, blocking collectives, local(): lax.all_gather(values[0], 'seq', axis=0, tiled=True)  39.2 us
    all_gather x1, blocking collectives, local(): lax.all_gather(keys[0], 'seq', axis=0, tiled=True)  26.7 us
  transfers between devices with their start and end apart: 3, of which 1 were waited for; matrix products, arithmetic and copies ran while one was open for 4% of the time, Pallas kernels for 0%

commit v1 on v0

v1 whole, which is shorter than its diff:
```python
import jax
import jax.numpy as jnp
from jax import lax
from jax.experimental import pallas as pl
from jax.experimental.pallas import tpu as pltpu
from jax.sharding import Mesh, PartitionSpec as P

HEAD = 128
TOK = 128
SPANS = 8
ZS = 32
WIDTH = 1536
HDM = 384
CHUNK = 1152
TAIL = WIDTH - CHUNK
SEQ = ("yl", "x")
F32 = jnp.float32
BF16 = jnp.bfloat16
VM = pl.BlockSpec(memory_space=pltpu.VMEM)
SM = pl.BlockSpec(memory_space=pltpu.SMEM)


def nt_dot(a, b):
    return lax.dot_general(a, b, (((1,), (1,)), ((), ())), preferred_element_type=F32)


def spread_kernel(w_ref, out_ref):
    w = w_ref[0].astype(F32)
    tail = w[:, CHUNK:]
    rows = [
        jnp.concatenate([tail[3 * r + s : 3 * r + s + 1] for s in range(3)], axis=1)
        for r in range(2)
    ]
    block = jnp.concatenate([w[:, :CHUNK]] + rows, axis=0).astype(BF16)
    for z in range(ZS):
        out_ref[z] = block


def attend_kernel(ts_ref, si_ref, q_ref, kv_ref, cot_ref, table_ref, keep_ref, send_ref, att_ref, gate_ref):
    place = lax.axis_index("yl") * 4 + lax.axis_index("x")
    core = lax.axis_index("c")
    limit = jnp.minimum(place, si_ref[0])
    inv_root = HEAD ** (-0.5)
    spans = lax.broadcasted_iota(jnp.int32, (1, SPANS * TOK), 1) // TOK
    visible = spans <= limit
    outs = []
    for h in range(HDM // HEAD):
        cols = slice(h * HEAD, (h + 1) * HEAD)
        keys = jnp.concatenate([kv_ref[j, :TOK, cols] for j in range(SPANS)], axis=0)
        values = jnp.concatenate([kv_ref[j, TOK:, cols] for j in range(SPANS)], axis=0)
        scores = nt_dot(q_ref[0, :, cols], keys) * inv_root
        scores = jnp.where(visible, scores, -jnp.inf)
        weights = jnp.exp(scores - jnp.max(scores, axis=1, keepdims=True))
        probs = (weights / jnp.sum(weights, axis=1, keepdims=True)).astype(BF16)
        outs.append(jnp.dot(probs, values, preferred_element_type=F32).astype(BF16))
    attended = jnp.concatenate(outs, axis=1)
    att_ref[...] = attended
    gate = table_ref[pl.ds(ts_ref[0], 1), :]
    gate_ref[...] = gate
    scaled = (gate * cot_ref[0].astype(F32)).astype(BF16)
    p = lax.broadcasted_iota(jnp.int32, (HDM, 1), 0)
    part = p // 192
    inner = (p // 64) % 3
    half = (p // 32) % 2
    feature = (((p % 32) * 2 + (part ^ core)) * 2 + half) * 3 + inner
    pick = (lax.broadcasted_iota(jnp.int32, (HDM, HDM), 1) == feature).astype(F32).astype(BF16)
    picked = nt_dot(pick, attended).astype(BF16)
    for part, ref in ((0, keep_ref), (1, send_ref)):
        for yl in range(2):
            rows = [
                jnp.dot(
                    picked[((part * 3 + i) * 2 + yl) * 32 : ((part * 3 + i) * 2 + yl + 1) * 32],
                    scaled,
                    preferred_element_type=F32,
                ).astype(ref.dtype)
                for i in range(3)
            ]
            ref[yl * 4 + 0] = rows[0][:, :1152]
            ref[yl * 4 + 1, :, :384] = rows[0][:, 1152:]
            ref[yl * 4 + 1, :, 384:] = rows[1][:, :768]
            ref[yl * 4 + 2, :, :768] = rows[1][:, 768:]
            ref[yl * 4 + 2, :, 768:] = rows[2][:, :384]
            ref[yl * 4 + 3] = rows[2][:, 384:]


def mix_kernel(att_ref, here_ref, there_ref, own_ref, send_ref):
    core = lax.axis_index("c")
    rank = lax.axis_index("yh")
    attended = jnp.concatenate(
        [att_ref[pl.ds(rank * 64, 64), :], att_ref[pl.ds((1 - rank) * 64, 64), :]], axis=0
    )
    p = lax.broadcasted_iota(jnp.int32, (1, 256), 1)
    z, r = p // 8, p % 8
    rows = lax.broadcasted_iota(jnp.int32, (HDM, 256), 0)
    head = jnp.zeros((TOK, CHUNK), F32)
    tail = jnp.zeros((TOK, TAIL), F32)
    for part, ref in ((0, here_ref), (1, there_ref)):
        base = (z * 2 + (part ^ core)) * 6

        def expand(feature):
            pick = (rows == feature).astype(F32).astype(BF16)
            return jnp.dot(attended, pick, preferred_element_type=F32).astype(BF16)

        block = ref[...]
        left = expand(jnp.where(r < 6, base + r, -1))
        head = head + jnp.dot(left, block, preferred_element_type=F32)
        for s in range(3):
            right = expand(jnp.where(r >= 6, base + 3 * (r - 6) + s, -1))
            tail = tail + jnp.dot(
                right, block[:, s * TAIL : (s + 1) * TAIL], preferred_element_type=F32
            )
    own_ref[:, :CHUNK] = head[:64]
    own_ref[:, CHUNK:] = tail[:64]
    send_ref[:, :CHUNK] = head[64:].astype(BF16)
    send_ref[:, CHUNK:] = tail[64:].astype(BF16)


def fold_kernel(parts_ref, out_ref):
    total = jnp.sum(parts_ref[...].astype(F32), axis=0).astype(BF16)
    out_ref[:, 0, :] = total[:, :640]
    out_ref[:, 1, :512] = total[:, 640:]
    out_ref[:, 1, 512:] = jnp.zeros((ZS, 128), BF16)


def local(queries, keys, values, proj_weight, gate_table, timestep, span_index, cotangent):
    def call(kernel, shapes, flops=0, nbytes=0):
        return pl.pallas_call(
            kernel,
            out_shape=shapes,
            in_specs=None,
            out_specs=jax.tree.map(lambda _: VM, shapes),
            cost_estimate=pl.CostEstimate(flops=flops, bytes_accessed=nbytes, transcendentals=0),
        )

    S = jax.ShapeDtypeStruct
    swap = [(0, 1), (1, 0)]
    with jax.named_scope("kv"):
        pair = jnp.concatenate([keys[0], values[0]], axis=0)
        pair = jnp.broadcast_to(pair[None], (SPANS,) + pair.shape)
        pairs = lax.all_to_all(pair, SEQ, 0, 0, tiled=True)
    with jax.named_scope("wz"):
        copies = pl.pallas_call(
            spread_kernel,
            out_shape=S((ZS, 8, CHUNK), BF16),
            in_specs=[VM],
            out_specs=VM,
        )(proj_weight)
        here = lax.all_to_all(copies, "z", 0, 0, tiled=True)
    with jax.named_scope("attend"):
        keep, send, attended, gate = pl.pallas_call(
            attend_kernel,
            out_shape=(
                S((SPANS, ZS, CHUNK), F32),
                S((SPANS, ZS, CHUNK), BF16),
                S((TOK, HDM), BF16),
                S((1, WIDTH), F32),
            ),
            in_specs=[SM, SM, VM, VM, VM, VM],
            out_specs=(VM, VM, VM, VM),
        )(timestep, span_index, queries, pairs, cotangent, gate_table)
    with jax.named_scope("cores"):
        other = lax.ppermute(send, "c", swap)
    with jax.named_scope("plane"):
        both = (keep + other.astype(F32)).astype(BF16)
        parts = lax.all_to_all(both, SEQ, 0, 0, tiled=True)
    with jax.named_scope("fold"):
        slices = pl.pallas_call(
            fold_kernel,
            out_shape=S((ZS, 2, 640), BF16),
            in_specs=[VM],
            out_specs=VM,
        )(parts)
    with jax.named_scope("depth"):
        last = lax.all_to_all(slices, "z", 0, 0, tiled=True)
        total = jnp.sum(last.astype(F32), axis=0).reshape(1280)[:CHUNK]
        weight_grad = total.reshape(1, 9, 128)
    with jax.named_scope("wc"):
        there = lax.ppermute(here, "c", swap)
    with jax.named_scope("mix"):
        own, away = pl.pallas_call(
            mix_kernel,
            out_shape=(S((64, WIDTH), F32), S((64, WIDTH), BF16)),
            in_specs=[VM, VM, VM],
            out_specs=(VM, VM),
        )(attended, here.reshape(256, CHUNK), there.reshape(256, CHUNK))
    with jax.named_scope("mp"):
        near = lax.ppermute(away, "yh", swap)
        output = (gate * (own + near.astype(F32))).astype(BF16)[None]
    return output, weight_grad


def solution(mesh):
    grid = Mesh(mesh.devices.reshape(ZS, 2, 2, 4, 2), ("z", "c", "yl", "x", "yh"))
    dp = ("z", "c")
    return jax.shard_map(
        local,
        mesh=grid,
        in_specs=(
            P(dp, SEQ, "yh"),
            P(dp, SEQ, "yh"),
            P(dp, SEQ, "yh"),
            P("yh", dp, None),
            P(),
            P(dp),
            P(dp),
            P(dp, SEQ, None),
        ),
        out_specs=(P(dp, SEQ + ("yh",), None), P("yh", dp + SEQ, None)),
        check_vma=False,
    )
```

time: 356 us -> 180 us (0.51)
  the two profiles are of different devices: /device:TPU:2 before, /device:TPU:16 now
where the time goes in v1:
time: 180 us; the launch traced here: 179 us
  waiting for transfers between devices  109 us (61%)
  starting transfers between devices  47.5 us (26%)
  Pallas kernels  11.4 us (6%)
  other arithmetic  4.98 us (3%)
  local copies, waits for them, and re-layouts  3.55 us (2%)
  between operations  2.04 us (1%)
    all_to_all x1, waiting for transfers between devices, local(): here = lax.all_to_all(copies, 'z', 0, 0, tiled=True)  57.9 us
    all_to_all x1, starting transfers between devices, local(): here = lax.all_to_all(copies, 'z', 0, 0, tiled=True)  28.7 us
    all_to_all x1, waiting for transfers between devices, local(): last = lax.all_to_all(slices, 'z', 0, 0, tiled=True)  20.9 us
    all_to_all x1, waiting for transfers between devices, local(): pairs = lax.all_to_all(pair, SEQ, 0, 0, tiled=True)  19.7 us
    all_to_all x1, waiting for transfers between devices, local(): parts = lax.all_to_all(both, SEQ, 0, 0, tiled=True)  8.64 us
    all_to_all x1, starting transfers between devices, local(): pairs = lax.all_to_all(pair, SEQ, 0, 0, tiled=True)  5.02 us
    pallas_call x1, Pallas kernels, local(): pl.pallas_call(attend_kernel, out_shape=(S((SPANS, ZS, CHUNK), F32), S((S...  4.84 us
    all_to_all x1, starting transfers between devices, local(): last = lax.all_to_all(slices, 'z', 0, 0, tiled=True)  3.81 us
  transfers between devices with their start and end apart: 7, of which 5 were waited for; matrix products, arithmetic and copies ran while one was open for 2% of the time, Pallas kernels for 6%

profile of v1, /device:TPU:16, one launch (start us, length us, event | category | flops | bytes accessed | tf_op | source)
XLA Modules:
  0.0 178.8 jit_solution(2656118374594165008)
XLA Ops:
  0.6 1.0 pad_maximum_fusion
  1.6 1.3 broadcast_in_dim.4
  2.9 5.0 %all-to-all-start = ((bf16[8,256,384]{2,1,0:T(8,128)(2,1)}), bf16[8,256,384]{2,1,0:T(8,128)(2,1)S(1)}, u32[]{:S(2)}, u32[]{:S(2)}) async-start(bf16[8,256,384]{2,1,0:T(8,128)(2,1)} %broadcast_in_dim.4), calls=%async_computation | async-start | bytes 3145728 | tf_op jit(solution)/shard_map/kv/all_to_all | solution.py:140
  7.9 1.6 wz.1
  9.5 19.7 %all-to-all-done.kv_ref = bf16[8,256,384]{2,1,0:T(8,128)(2,1)S(1)} async-done(((bf16[8,256,384]{2,1,0:T(8,128)(2,1)}), bf16[8,256,384]{2,1,0:T(8,128)(2,1)S(1)}, u32[]{:S(2)}, u32[]{:S(2)}) %all-to-all-start) | async-done | bytes 1572896 | tf_op jit(solution)/shard_map/kv/all_to_all | solution.py:140
  29.2 0.0 copy-start
  29.2 28.7 %all-to-all-start.1 = ((bf16[32,8,1152]{2,1,0:T(8,128)(2,1)}), bf16[32,8,1152]{2,1,0:T(8,128)(2,1)S(1)}, u32[]{:S(2)}, u32[]{:S(2)}) async-start(bf16[32,8,1152]{2,1,0:T(8,128)(2,1)} %wz.1), calls=%async_computation.1 | async-start | bytes 1179648 | tf_op jit(solution)/shard_map/wz/all_to_all | solution.py:148
  59.3 0.0 copy-done
  59.3 4.8 %attend.1 = (f32[8,32,1152]{2,1,0:T(8,128)}, bf16[8,32,1152]{2,1,0:T(8,128)(2,1)}, bf16[128,384]{1,0:T(8,128)(2,1)}, f32[1,1536]{1,0:T(1,128)}) custom-call(s32[1]{0:T(128)S(6)} %copy.10.ts_ref, s32[1]{0:T(128)S(6)} %copy.11.si_ref, bf16[1,128,384]{2,1,0:T(8,128)(2,1)} %q_ref.1, bf16[8,256,384]{2,1,0:T(8,128)(2,1)} %copy-done, ...), custom_call_target="tpu_custom_call" | custom-call | tf_op jit(solution)/shard_map/attend/pallas_call | solution.py:150
  64.1 1.9 %collective-permute-start.2 = (bf16[8,32,1152]{2,1,0:T(8,128)(2,1)}, bf16[8,32,1152]{2,1,0:T(8,128)(2,1)S(1)}, u32[]{:S(2)}, u32[]{:S(2)}) collective-permute-start(bf16[8,32,1152]{2,1,0:T(8,128)(2,1)} %get-tuple-element.13), channel_id=1, source_target_pairs={{0,16},{16,0},{1,17},{17,1},{2,18},{18,2},{3,19},{19,3},{4,20},{20... | collective-permute-start | bytes 1769480 | tf_op jit(solution)/shard_map/cores/ppermute | solution.py:162
  66.0 2.2 %collective-permute-done.2 = bf16[8,32,1152]{2,1,0:T(8,128)(2,1)S(1)} collective-permute-done((bf16[8,32,1152]{2,1,0:T(8,128)(2,1)}, bf16[8,32,1152]{2,1,0:T(8,128)(2,1)S(1)}, u32[]{:S(2)}, u32[]{:S(2)}) %collective-permute-start.2) | collective-permute-done | bytes 589856 | tf_op jit(solution)/shard_map/cores/ppermute | solution.py:162
  68.2 2.2 %add_convert_fusion = bf16[8,32,1152]{2,1,0:T(8,128)(2,1)} fusion(f32[8,32,1152]{2,1,0:T(8,128)} %get-tuple-element.12, bf16[8,32,1152]{2,1,0:T(8,128)(2,1)S(1)} %collective-permute-done.2), kind=kLoop, calls=%fused_computation | loop fusion | flops 884736 | bytes 2359296 | tf_op jit(solution)/shard_map/plane/convert_element_type | solution.py:164
  70.4 57.9 %all-to-all-done.1 = bf16[32,8,1152]{2,1,0:T(8,128)(2,1)S(1)} async-done(((bf16[32,8,1152]{2,1,0:T(8,128)(2,1)}), bf16[32,8,1152]{2,1,0:T(8,128)(2,1)S(1)}, u32[]{:S(2)}, u32[]{:S(2)}) %all-to-all-start.1) | async-done | bytes 589856 | tf_op jit(solution)/shard_map/wz/all_to_all | solution.py:148
  128.3 0.0 copy-start.1
  128.3 3.5 %all-to-all-start.2 = ((bf16[8,32,1152]{2,1,0:T(8,128)(2,1)}), bf16[8,32,1152]{2,1,0:T(8,128)(2,1)S(1)}, u32[]{:S(2)}, u32[]{:S(2)}) async-start(bf16[8,32,1152]{2,1,0:T(8,128)(2,1)} %add_convert_fusion), calls=%async_computation.2 | async-start | bytes 1179648 | tf_op jit(solution)/shard_map/plane/all_to_all | solution.py:165
  131.8 0.0 copy-start.4
  131.8 1.9 %collective-permute-start = (bf16[32,8,1152]{2,1,0:T(8,128)(2,1)S(1)}, bf16[32,8,1152]{2,1,0:T(8,128)(2,1)S(1)}, u32[]{:S(2)}, u32[]{:S(2)}) collective-permute-start(bf16[32,8,1152]{2,1,0:T(8,128)(2,1)S(1)} %all-to-all-done.1), channel_id=1, source_target_pairs={{0,16},{16,0},{1,17},{17,1},{2,18},{18,2},{3,19},{19,3},{4,20},{20... | collective-permute-start | bytes 1769480 | tf_op jit(solution)/shard_map/wc/ppermute | solution.py:178
  133.8 8.6 %all-to-all-done.2.parts_ref = bf16[8,32,1152]{2,1,0:T(8,128)(2,1)S(1)} async-done(((bf16[8,32,1152]{2,1,0:T(8,128)(2,1)}), bf16[8,32,1152]{2,1,0:T(8,128)(2,1)S(1)}, u32[]{:S(2)}, u32[]{:S(2)}) %all-to-all-start.2) | async-done | bytes 589856 | tf_op jit(solution)/shard_map/plane/all_to_all | solution.py:165
  142.4 0.0 copy-start.2
  142.4 0.8 copy-done.2
  143.2 1.8 %fold.1 = bf16[32,2,640]{2,1,0:T(2,128)(2,1)} custom-call(bf16[8,32,1152]{2,1,0:T(8,128)(2,1)} %copy-done.2), custom_call_target="tpu_custom_call" | custom-call | tf_op jit(solution)/shard_map/fold/pallas_call | solution.py:167
  145.1 3.8 %all-to-all-start.3 = ((bf16[32,2,640]{2,1,0:T(2,128)(2,1)}), bf16[32,2,640]{2,1,0:T(2,128)(2,1)S(1)}, u32[]{:S(2)}, u32[]{:S(2)}) async-start(bf16[32,2,640]{2,1,0:T(2,128)(2,1)} %fold.1), calls=%async_computation.3 | async-start | bytes 163840 | tf_op jit(solution)/shard_map/depth/all_to_all | solution.py:174
  148.9 0.0 collective-permute-done
  148.9 0.0 copy-start.3
  148.9 0.0 copy-done.1
  148.9 0.8 copy-done.3
  149.7 3.2 %mix.1 = (f32[64,1536]{1,0:T(8,128)}, bf16[64,1536]{1,0:T(8,128)(2,1)}) custom-call(bf16[128,384]{1,0:T(8,128)(2,1)} %get-tuple-element.9.att_ref, bf16[256,1152]{1,0:T(8,128)(2,1)} %bitcast.7, bf16[256,1152]{1,0:T(8,128)(2,1)} %bitcast.8), custom_call_target="tpu_custom_call" | custom-call | tf_op jit(solution)/shard_map/mix/pallas_call | solution.py:180
  152.9 2.5 %collective-permute-start.1 = (bf16[64,1536]{1,0:T(8,128)(2,1)}, bf16[64,1536]{1,0:T(8,128)(2,1)S(1)}, u32[]{:S(2)}, u32[]{:S(2)}) collective-permute-start(bf16[64,1536]{1,0:T(8,128)(2,1)} %get-tuple-element.11), channel_id=1, source_target_pairs={{0,1},{1,0},{2,3},{3,2},{4,5},{5,4},{6,7},{7,6},{8,9},{9,8},{10,11... | collective-permute-start | bytes 589832 | tf_op jit(solution)/shard_map/mp/ppermute | solution.py:187
  155.4 0.0 copy-done.4
  155.4 20.9 %all-to-all-done.3 = bf16[32,2,640]{2,1,0:T(2,128)(2,1)S(1)} async-done(((bf16[32,2,640]{2,1,0:T(2,128)(2,1)}), bf16[32,2,640]{2,1,0:T(2,128)(2,1)S(1)}, u32[]{:S(2)}, u32[]{:S(2)}) %all-to-all-start.3) | async-done | bytes 81952 | tf_op jit(solution)/shard_map/depth/all_to_all | solution.py:174
  176.4 0.1 convert_reduce_fusion
  176.5 0.6 reshape.20
  177.1 0.0 collective-permute-done.1
  177.1 1.7 fusion
  (2 shorter events, 0.0 us)
Async XLA Ops:
  2.9 26.3 %all-to-all-start = ((bf16[8,256,384]{2,1,0:T(8,128)(2,1)}), bf16[8,256,384]{2,1,0:T(8,128)(2,1)S(1)}, u32[]{:S(2)}, u32[]{:S(2)}) async-start(bf16[8,256,384]{2,1,0:T(8,128)(2,1)} %broadcast_in_dim.4), calls=%async_computation | async-start | bytes 3145728 | tf_op jit(solution)/shard_map/kv/all_to_all | solution.py:140
  29.2 30.0 %copy-start = (bf16[8,256,384]{2,1,0:T(8,128)(2,1)}, bf16[8,256,384]{2,1,0:T(8,128)(2,1)S(1)}, u32[]{:S(2)}) copy-start(bf16[8,256,384]{2,1,0:T(8,128)(2,1)S(1)} %all-to-all-done.kv_ref) | copy-start | bytes 4718596
  29.2 99.0 %all-to-all-start.1 = ((bf16[32,8,1152]{2,1,0:T(8,128)(2,1)}), bf16[32,8,1152]{2,1,0:T(8,128)(2,1)S(1)}, u32[]{:S(2)}, u32[]{:S(2)}) async-start(bf16[32,8,1152]{2,1,0:T(8,128)(2,1)} %wz.1), calls=%async_computation.1 | async-start | bytes 1179648 | tf_op jit(solution)/shard_map/wz/all_to_all | solution.py:148
  64.1 4.1 %collective-permute-start.2 = (bf16[8,32,1152]{2,1,0:T(8,128)(2,1)}, bf16[8,32,1152]{2,1,0:T(8,128)(2,1)S(1)}, u32[]{:S(2)}, u32[]{:S(2)}) collective-permute-start(bf16[8,32,1152]{2,1,0:T(8,128)(2,1)} %get-tuple-element.13), channel_id=1, source_target_pairs={{0,16},{16,0},{1,17},{17,1},{2,18},{18,2},{3,19},{19,3},{4,20},{20... | collective-permute-start | bytes 1769480 | tf_op jit(solution)/shard_map/cores/ppermute | solution.py:162
  128.3 20.6 %copy-start.1 = (bf16[32,8,1152]{2,1,0:T(8,128)(2,1)}, bf16[32,8,1152]{2,1,0:T(8,128)(2,1)S(1)}, u32[]{:S(2)}) copy-start(bf16[32,8,1152]{2,1,0:T(8,128)(2,1)S(1)} %all-to-all-done.1) | copy-start | bytes 1769476
  128.3 14.1 %all-to-all-start.2 = ((bf16[8,32,1152]{2,1,0:T(8,128)(2,1)}), bf16[8,32,1152]{2,1,0:T(8,128)(2,1)S(1)}, u32[]{:S(2)}, u32[]{:S(2)}) async-start(bf16[8,32,1152]{2,1,0:T(8,128)(2,1)} %add_convert_fusion), calls=%async_computation.2 | async-start | bytes 1179648 | tf_op jit(solution)/shard_map/plane/all_to_all | solution.py:165
  131.8 23.6 %copy-start.4 = (f32[1,1536]{1,0:T(1,128)S(1)}, f32[1,1536]{1,0:T(1,128)}, u32[]{:S(2)}) copy-start(f32[1,1536]{1,0:T(1,128)} %get-tuple-element.8) | copy-start | bytes 18436
  131.8 17.1 %collective-permute-start = (bf16[32,8,1152]{2,1,0:T(8,128)(2,1)S(1)}, bf16[32,8,1152]{2,1,0:T(8,128)(2,1)S(1)}, u32[]{:S(2)}, u32[]{:S(2)}) collective-permute-start(bf16[32,8,1152]{2,1,0:T(8,128)(2,1)S(1)} %all-to-all-done.1), channel_id=1, source_target_pairs={{0,16},{16,0},{1,17},{17,1},{2,18},{18,2},{3,19},{19,3},{4,20},{20... | collective-permute-start | bytes 1769480 | tf_op jit(solution)/shard_map/wc/ppermute | solution.py:178
  142.4 0.8 copy-start.2
  145.1 31.3 %all-to-all-start.3 = ((bf16[32,2,640]{2,1,0:T(2,128)(2,1)}), bf16[32,2,640]{2,1,0:T(2,128)(2,1)S(1)}, u32[]{:S(2)}, u32[]{:S(2)}) async-start(bf16[32,2,640]{2,1,0:T(2,128)(2,1)} %fold.1), calls=%async_computation.3 | async-start | bytes 163840 | tf_op jit(solution)/shard_map/depth/all_to_all | solution.py:174
  148.9 0.8 copy-start.3
  152.9 24.2 %collective-permute-start.1 = (bf16[64,1536]{1,0:T(8,128)(2,1)}, bf16[64,1536]{1,0:T(8,128)(2,1)S(1)}, u32[]{:S(2)}, u32[]{:S(2)}) collective-permute-start(bf16[64,1536]{1,0:T(8,128)(2,1)} %get-tuple-element.11), channel_id=1, source_target_pairs={{0,1},{1,0},{2,3},{3,2},{4,5},{5,4},{6,7},{7,6},{8,9},{9,8},{10,11... | collective-permute-start | bytes 589832 | tf_op jit(solution)/shard_map/mp/ppermute | solution.py:187

commit v2 on v1

v2 whole, which is shorter than its diff:
```python
import jax
import jax.numpy as jnp
from jax import lax
from jax.experimental import pallas as pl
from jax.experimental.pallas import tpu as pltpu
from jax.sharding import Mesh, PartitionSpec as P


HEAD = 128
TOK = 128
SPANS = 8
ZS = 32
WIDTH = 1536
HDM = 384
CHUNK = 1152
TAIL = WIDTH - CHUNK
SEQ = ("yl", "x")
F32 = jnp.float32
BF16 = jnp.bfloat16
VM = pl.BlockSpec(memory_space=pltpu.VMEM)
SM = pl.BlockSpec(memory_space=pltpu.SMEM)


def nt_dot(a, b):
    return lax.dot_general(a, b, (((1,), (1,)), ((), ())), preferred_element_type=F32)


def scale_kernel(ts_ref, cot_ref, table_ref, scaled_ref, gate_ref):
    gate = table_ref[pl.ds(ts_ref[0], 1), :]
    gate_ref[...] = gate
    scaled_ref[...] = (gate * cot_ref[0].astype(F32)).astype(BF16)


def attend_kernel(si_ref, q_ref, kv_ref, scaled_ref, keep_ref, send_ref, att_ref):
    place = lax.axis_index("yl") * 4 + lax.axis_index("x")
    core = lax.axis_index("c")
    limit = jnp.minimum(place, si_ref[0])
    inv_root = HEAD ** (-0.5)
    spans = lax.broadcasted_iota(jnp.int32, (1, SPANS * TOK), 1) // TOK
    visible = spans <= limit
    outs = []
    for h in range(HDM // HEAD):
        cols = slice(h * HEAD, (h + 1) * HEAD)
        keys = jnp.concatenate([kv_ref[j, :TOK, cols] for j in range(SPANS)], axis=0)
        values = jnp.concatenate([kv_ref[j, TOK:, cols] for j in range(SPANS)], axis=0)
        scores = nt_dot(q_ref[0, :, cols], keys) * inv_root
        scores = jnp.where(visible, scores, -jnp.inf)
        weights = jnp.exp(scores - jnp.max(scores, axis=1, keepdims=True))
        probs = (weights / jnp.sum(weights, axis=1, keepdims=True)).astype(BF16)
        outs.append(jnp.dot(probs, values, preferred_element_type=F32).astype(BF16))
    attended = jnp.concatenate(outs, axis=1)
    att_ref[...] = attended
    scaled = scaled_ref[...]
    p = lax.broadcasted_iota(jnp.int32, (HDM, 1), 0)
    part = p // 192
    inner = (p // 64) % 3
    half = (p // 32) % 2
    feature = (((p % 32) * 2 + (part ^ core)) * 2 + half) * 3 + inner
    pick = (lax.broadcasted_iota(jnp.int32, (HDM, HDM), 1) == feature).astype(F32).astype(BF16)
    picked = nt_dot(pick, attended).astype(BF16)
    for part, ref in ((0, keep_ref), (1, send_ref)):
        for yl in range(2):
            rows = [
                jnp.dot(
                    picked[((part * 3 + i) * 2 + yl) * 32 : ((part * 3 + i) * 2 + yl + 1) * 32],
                    scaled,
                    preferred_element_type=F32,
                ).astype(ref.dtype)
                for i in range(3)
            ]
            ref[yl * 4 + 0] = rows[0][:, :1152]
            ref[yl * 4 + 1, :, :384] = rows[0][:, 1152:]
            ref[yl * 4 + 1, :, 384:] = rows[1][:, :768]
            ref[yl * 4 + 2, :, :768] = rows[1][:, 768:]
            ref[yl * 4 + 2, :, 768:] = rows[2][:, :384]
            ref[yl * 4 + 3] = rows[2][:, 384:]


def merge_kernel(keep_ref, other_ref, near_ref, far_ref, out_ref):
    rows = jnp.concatenate([near_ref[...].astype(F32), far_ref[...].astype(F32)], axis=0)
    tails = [
        jnp.concatenate([rows[3 * q + s : 3 * q + s + 1, CHUNK:] for s in range(3)], axis=1)
        for q in range(8)
    ]
    block = jnp.concatenate([rows[:, :CHUNK]] + tails, axis=0).astype(BF16)
    for j in range(SPANS):
        out_ref[j, :ZS] = (keep_ref[j] + other_ref[j].astype(F32)).astype(BF16)
        out_ref[j, ZS:] = block


def expand_kernel(att_ref, out_ref):
    core = lax.axis_index("c")
    depth = lax.axis_index("z")
    attended = att_ref[...]
    p = lax.broadcasted_iota(jnp.int32, (1, 256), 1)
    place, r = p // 32, p % 32
    rows = lax.broadcasted_iota(jnp.int32, (HDM, 256), 0)
    for part in range(2):
        side = part ^ core
        for kind in range(4):
            row = r if kind == 0 else 3 * (r - 24) + kind - 1
            z = (depth + side * 8 + place - 8 + 16 * (row // 12) + ZS) % ZS
            t = row % 12
            feature = (z * 2 + ((t // 6) ^ side)) * 6 + t % 6
            feature = jnp.where((r < 24) == (kind == 0), feature, -1)
            pick = (rows == feature).astype(F32).astype(BF16)
            out_ref[part, kind] = jnp.dot(attended, pick, preferred_element_type=F32).astype(BF16)


def mix_kernel(wide_ref, here_ref, there_ref, own_ref, send_ref):
    rank = lax.axis_index("yh")
    head = jnp.zeros((TOK, CHUNK), F32)
    tail = jnp.zeros((TOK, TAIL), F32)
    for part, ref in ((0, here_ref), (1, there_ref)):
        block = ref[...].reshape(256, CHUNK)
        head = head + jnp.dot(wide_ref[part, 0], block, preferred_element_type=F32)
        for s in range(3):
            tail = tail + jnp.dot(
                wide_ref[part, 1 + s],
                block[:, s * TAIL : (s + 1) * TAIL],
                preferred_element_type=F32,
            )
    first = rank == 0
    for cols, m in ((slice(0, CHUNK), head), (slice(CHUNK, WIDTH), tail)):
        own_ref[:, cols] = jnp.where(first, m[:64], m[64:])
        send_ref[:, cols] = jnp.where(first, m[64:], m[:64]).astype(BF16)


def fold_kernel(parts_ref, out_ref, here_ref):
    total = parts_ref[0, :ZS].astype(F32)
    for j in range(1, SPANS):
        total = total + parts_ref[j, :ZS].astype(F32)
    total = total.astype(BF16)
    out_ref[:, 0, :] = total[:, :640]
    out_ref[:, 1, :512] = total[:, 640:]
    out_ref[:, 1, 512:] = jnp.zeros((ZS, 128), BF16)
    for j in range(SPANS):
        here_ref[j] = parts_ref[j, ZS:]


def columns(shift):
    pairs = []
    for z in range(ZS):
        for c in range(2):
            for s in range(SPANS):
                source = (z + c * 8 + s - 8 + shift) % ZS
                pairs.append(((source * 2 + c) * SPANS + s, (z * 2 + c) * SPANS + s))
    return pairs


def vmem(mib):
    return pltpu.CompilerParams(vmem_limit_bytes=mib << 20)


def local(queries, keys, values, proj_weight, gate_table, timestep, span_index, cotangent):
    S = jax.ShapeDtypeStruct
    swap = [(0, 1), (1, 0)]
    pair = jnp.concatenate([keys[0], values[0]], axis=0)
    pair = jnp.broadcast_to(pair[None], (SPANS,) + pair.shape)
    pairs = lax.all_to_all(pair, SEQ, 0, 0, tiled=True)
    every = ("z", "c") + SEQ
    mate = lax.ppermute(proj_weight[0], "c", swap)
    dozen = jnp.concatenate([proj_weight[0], mate], axis=0)
    far = lax.ppermute(dozen, every, columns(16))
    near = lax.ppermute(dozen, every, columns(0))
    scaled, gate = pl.pallas_call(
        scale_kernel,
        out_shape=(S((TOK, WIDTH), BF16), S((1, WIDTH), F32)),
        in_specs=[SM, VM, VM],
        out_specs=(VM, VM),
        compiler_params=vmem(8),
    )(timestep, cotangent, gate_table)
    keep, send, attended = pl.pallas_call(
        attend_kernel,
        out_shape=(S((SPANS, ZS, CHUNK), F32), S((SPANS, ZS, CHUNK), BF16), S((TOK, HDM), BF16)),
        in_specs=[SM, VM, VM, VM],
        out_specs=(VM, VM, VM),
        compiler_params=vmem(20),
    )(span_index, queries, pairs, scaled)
    other = lax.ppermute(send, "c", swap)
    both = pl.pallas_call(
        merge_kernel,
        out_shape=S((SPANS, 2 * ZS, CHUNK), BF16),
        in_specs=[VM, VM, VM, VM],
        out_specs=VM,
        compiler_params=vmem(8),
    )(keep, other, near, far)
    parts = lax.all_to_all(both, SEQ, 0, 0, tiled=True)
    wide = pl.pallas_call(
        expand_kernel,
        out_shape=S((2, 4, TOK, 256), BF16),
        in_specs=[VM],
        out_specs=VM,
        compiler_params=vmem(8),
    )(attended)
    slices, here = pl.pallas_call(
        fold_kernel,
        out_shape=(S((ZS, 2, 640), BF16), S((SPANS, ZS, CHUNK), BF16)),
        in_specs=[VM],
        out_specs=(VM, VM),
        compiler_params=vmem(8),
    )(parts)
    last = lax.all_to_all(slices, "z", 0, 0, tiled=True)
    total = jnp.sum(last.astype(F32), axis=0).reshape(1280)[:CHUNK]
    weight_grad = total.reshape(1, 9, 128)
    there = lax.ppermute(here, "c", swap)
    own, away = pl.pallas_call(
        mix_kernel,
        out_shape=(S((64, WIDTH), F32), S((64, WIDTH), BF16)),
        in_specs=[VM, VM, VM],
        out_specs=(VM, VM),
        compiler_params=vmem(12),
    )(wide, here, there)
    rest = lax.ppermute(away, "yh", swap)
    output = (gate * (own + rest.astype(F32))).astype(BF16)[None]
    return output, weight_grad


def solution(mesh):
    grid = Mesh(mesh.devices.reshape(ZS, 2, 2, 4, 2), ("z", "c", "yl", "x", "yh"))
    dp = ("z", "c")
    return jax.shard_map(
        local,
        mesh=grid,
        in_specs=(
            P(dp, SEQ, "yh"),
            P(dp, SEQ, "yh"),
            P(dp, SEQ, "yh"),
            P("yh", dp, None),
            P(),
            P(dp),
            P(dp),
            P(dp, SEQ, None),
        ),
        out_specs=(P(dp, SEQ + ("yh",), None), P("yh", dp + SEQ, None)),
        check_vma=False,
    )
```

time: 180 us -> 146 us (0.81)
  the two profiles are of different devices: /device:TPU:16 before, /device:TPU:1 now
where the time goes in v2:
time: 146 us; the launch traced here: 145 us
  starting transfers between devices  71.2 us (49%)
  waiting for transfers between devices  35.3 us (24%)
  blocking collectives  28.4 us (19%)
  Pallas kernels  4.49 us (3%)
  between operations  2.09 us (1%)
  local copies, waits for them, and re-layouts  1.94 us (1%)
  other arithmetic  1.82 us (1%)
    all_to_all x1, blocking collectives, local(): parts = lax.all_to_all(both, SEQ, 0, 0, tiled=True)  28.4 us
    ppermute x1, starting transfers between devices, local(): far = lax.ppermute(dozen, every, columns(16))  24.9 us
    all_to_all x1, waiting for transfers between devices, local(): last = lax.all_to_all(slices, 'z', 0, 0, tiled=True)  20.8 us
    all_to_all x1, starting transfers between devices, local(): last = lax.all_to_all(slices, 'z', 0, 0, tiled=True)  16.5 us
    ppermute x1, starting transfers between devices, local(): other = lax.ppermute(send, 'c', swap)  14.8 us
    all_to_all x1, waiting for transfers between devices, local(): pairs = lax.all_to_all(pair, SEQ, 0, 0, tiled=True)  11.8 us
    all_to_all x1, starting transfers between devices, local(): pairs = lax.all_to_all(pair, SEQ, 0, 0, tiled=True)  5.98 us
    ppermute x1, starting transfers between devices, local(): rest = lax.ppermute(away, 'yh', swap)  4.53 us
  transfers between devices with their start and end apart: 8, of which 4 were waited for; matrix products, arithmetic and copies ran while one was open for 1% of the time, Pallas kernels for 1%

profile of v2, /device:TPU:1, one launch (start us, length us, event | category | flops | bytes accessed | tf_op | source)
XLA Modules:
  0.0 145.2 jit_solution(2417573167054601501)
XLA Ops:
  0.6 1.0 pad_maximum_fusion
  1.6 1.3 broadcast_in_dim.4
  2.9 0.0 copy-start
  2.9 0.0 copy-start.2
  2.9 0.0 copy-start.1
  2.9 6.0 %all-to-all-start = ((bf16[8,256,384]{2,1,0:T(8,128)(2,1)}), bf16[8,256,384]{2,1,0:T(8,128)(2,1)S(1)}, u32[]{:S(2)}, u32[]{:S(2)}) async-start(bf16[8,256,384]{2,1,0:T(8,128)(2,1)} %broadcast_in_dim.4), calls=%async_computation | async-start | bytes 3145728 | tf_op jit(solution)/shard_map/all_to_all | solution.py:160
  10.2 0.0 copy-done
  10.2 0.0 copy-done.2
  10.2 0.0 copy-start.3
  10.2 0.1 shard_map.95
  10.3 11.8 %all-to-all-done.kv_ref = bf16[8,256,384]{2,1,0:T(8,128)(2,1)S(1)} async-done(((bf16[8,256,384]{2,1,0:T(8,128)(2,1)}), bf16[8,256,384]{2,1,0:T(8,128)(2,1)S(1)}, u32[]{:S(2)}, u32[]{:S(2)}) %all-to-all-start) | async-done | bytes 1572896 | tf_op jit(solution)/shard_map/all_to_all | solution.py:160
  22.1 0.0 copy-done.1
  22.1 2.4 %shard_map.96 = (f32[8,32,1152]{2,1,0:T(8,128)S(1)}, bf16[8,32,1152]{2,1,0:T(8,128)(2,1)S(1)}, bf16[128,384]{1,0:T(8,128)(2,1)S(1)}) custom-call(s32[1]{0:T(128)S(6)} %copy.11.si_ref, bf16[1,128,384]{2,1,0:T(8,128)(2,1)S(1)} %copy-done.1, bf16[8,256,384]{2,1,0:T(8,128)(2,1)S(1)} %all-to-all-done.kv_ref, bf16[128,1536]{1,0:T(8,128)(2,1)S(1)} %get-tuple-element.12.scaled_ref), custom_call_target="tpu_custom_call" | custom-call | tf_op jit(solution)/shard_map/pallas_call | solution.py:173
  24.4 14.8 %collective-permute-start = (bf16[8,32,1152]{2,1,0:T(8,128)(2,1)S(1)}, bf16[8,32,1152]{2,1,0:T(8,128)(2,1)S(1)}, u32[]{:S(2)}, u32[]{:S(2)}) collective-permute-start(bf16[8,32,1152]{2,1,0:T(8,128)(2,1)S(1)} %get-tuple-element.15), channel_id=1, source_target_pairs={{0,16},{16,0},{1,17},{17,1},{2,18},{18,2},{3,19},{19,3},{4,20},{20... | collective-permute-start | bytes 1769480 | tf_op jit(solution)/shard_map/ppermute | solution.py:180
  39.3 0.0 copy-done.3
  39.3 1.9 %collective-permute-start.1 = (bf16[6,1536]{1,0:T(8,128)(2,1)S(1)}, bf16[6,1536]{1,0:T(8,128)(2,1)S(1)}, u32[]{:S(2)}, u32[]{:S(2)}) collective-permute-start(bf16[6,1536]{1,0:T(8,128)(2,1)S(1)} %bitcast.9), channel_id=1, source_target_pairs={{0,16},{16,0},{1,17},{17,1},{2,18},{18,2},{3,19},{19,3},{4,20},{20... | collective-permute-start | bytes 55304 | tf_op jit(solution)/shard_map/ppermute | solution.py:162
  41.2 1.2 collective-permute-done.1
  42.4 0.7 collective-permute-start.2
  43.1 24.9 %collective-permute-start.3 = (bf16[12,1536]{1,0:T(8,128)(2,1)S(1)}, bf16[12,1536]{1,0:T(8,128)(2,1)S(1)}, u32[]{:S(2)}, u32[]{:S(2)}) collective-permute-start(bf16[12,1536]{1,0:T(8,128)(2,1)S(1)} %pad_maximum_fusion.1), channel_id=1, source_target_pairs={{256,0},{290,2},{324,4},{358,6},{392,8},{426,10},{460,12},{494,14}... | collective-permute-start | bytes 110600 | tf_op jit(solution)/shard_map/ppermute | solution.py:164
  68.0 0.0 collective-permute-done.2.near_ref
  68.0 1.6 %collective-permute-done.3.far_ref = bf16[12,1536]{1,0:T(8,128)(2,1)S(1)} collective-permute-done((bf16[12,1536]{1,0:T(8,128)(2,1)S(1)}, bf16[12,1536]{1,0:T(8,128)(2,1)S(1)}, u32[]{:S(2)}, u32[]{:S(2)}) %collective-permute-start.3) | collective-permute-done | bytes 36896 | tf_op jit(solution)/shard_map/ppermute | solution.py:164
  69.5 0.0 collective-permute-done.other_ref
  69.5 0.2 shard_map.98
  69.7 28.4 %all_to_all.15.parts_ref = bf16[8,64,1152]{2,1,0:T(8,128)(2,1)S(1)} all-to-all(bf16[8,64,1152]{2,1,0:T(8,128)(2,1)S(1)} %shard_map.98), channel_id=1, replica_groups=mesh['z'=32,'c'=2,'yl'=2,'x'=4,'yh'=2] {'yl','x'}, dimensions={0} | all-to-all | bytes 2359296 | tf_op jit(solution)/shard_map/all_to_all | solution.py:188
  98.1 0.8 shard_map.99
  98.9 1.9 %collective-permute-start.4 = (bf16[8,32,1152]{2,1,0:T(8,128)(2,1)S(1)}, bf16[8,32,1152]{2,1,0:T(8,128)(2,1)S(1)}, u32[]{:S(2)}, u32[]{:S(2)}) collective-permute-start(bf16[8,32,1152]{2,1,0:T(8,128)(2,1)S(1)} %get-tuple-element.16.here_ref), channel_id=1, source_target_pairs={{0,16},{16,0},{1,17},{17,1},{2,18},{18,2},{3,19},{19,3},{4,20},{20... | collective-permute-start | bytes 1769480 | tf_op jit(solution)/shard_map/ppermute | solution.py:206
  100.8 16.5 %all-to-all-start.2 = ((bf16[32,2,640]{2,1,0:T(2,128)(2,1)}), bf16[32,2,640]{2,1,0:T(2,128)(2,1)S(1)}, u32[]{:S(2)}, u32[]{:S(2)}) async-start(bf16[32,2,640]{2,1,0:T(2,128)(2,1)} %get-tuple-element.19), calls=%async_computation.2 | async-start | bytes 163840 | tf_op jit(solution)/shard_map/all_to_all | solution.py:203
  117.3 0.5 shard_map.97.wide_ref
  117.8 0.0 collective-permute-done.4.there_ref
  117.9 0.5 shard_map.100
  118.4 4.5 %collective-permute-start.5 = (bf16[64,1536]{1,0:T(8,128)(2,1)S(1)}, bf16[64,1536]{1,0:T(8,128)(2,1)S(1)}, u32[]{:S(2)}, u32[]{:S(2)}) collective-permute-start(bf16[64,1536]{1,0:T(8,128)(2,1)S(1)} %get-tuple-element.18), channel_id=1, source_target_pairs={{0,1},{1,0},{2,3},{3,2},{4,5},{5,4},{6,7},{7,6},{8,9},{9,8},{10,11... | collective-permute-start | bytes 589832 | tf_op jit(solution)/shard_map/ppermute | solution.py:214
  123.0 20.8 %all-to-all-done.2 = bf16[32,2,640]{2,1,0:T(2,128)(2,1)S(1)} async-done(((bf16[32,2,640]{2,1,0:T(2,128)(2,1)}), bf16[32,2,640]{2,1,0:T(2,128)(2,1)S(1)}, u32[]{:S(2)}, u32[]{:S(2)}) %all-to-all-start.2) | async-done | bytes 81952 | tf_op jit(solution)/shard_map/all_to_all | solution.py:203
  143.8 0.1 convert_reduce_fusion
  143.9 0.6 reshape.12
  144.5 0.0 collective-permute-done.5
  144.5 0.7 fusion
  (3 shorter events, 0.1 us)
Async XLA Ops:
  2.9 7.3 %copy-start = (bf16[1,128,1536]{2,1,0:T(8,128)(2,1)S(1)}, bf16[1,128,1536]{2,1,0:T(8,128)(2,1)}, u32[]{:S(2)}) copy-start(bf16[1,128,1536]{2,1,0:T(8,128)(2,1)} %cot_ref.1) | copy-start | bytes 1179652
  2.9 7.3 %copy-start.2 = (f32[4,1536]{1,0:T(4,128)S(1)}, f32[4,1536]{1,0:T(4,128)}, u32[]{:S(2)}) copy-start(f32[4,1536]{1,0:T(4,128)} %table_ref.1) | copy-start | bytes 73732
  2.9 19.1 %copy-start.1 = (bf16[1,128,384]{2,1,0:T(8,128)(2,1)S(1)}, bf16[1,128,384]{2,1,0:T(8,128)(2,1)}, u32[]{:S(2)}) copy-start(bf16[1,128,384]{2,1,0:T(8,128)(2,1)} %q_ref.1) | copy-start | bytes 294916
  2.9 19.1 %all-to-all-start = ((bf16[8,256,384]{2,1,0:T(8,128)(2,1)}), bf16[8,256,384]{2,1,0:T(8,128)(2,1)S(1)}, u32[]{:S(2)}, u32[]{:S(2)}) async-start(bf16[8,256,384]{2,1,0:T(8,128)(2,1)} %broadcast_in_dim.4), calls=%async_computation | async-start | bytes 3145728 | tf_op jit(solution)/shard_map/all_to_all | solution.py:160
  10.2 29.1 %copy-start.3 = (bf16[1,6,1536]{2,1,0:T(8,128)(2,1)S(1)}, bf16[1,6,1536]{2,1,0:T(8,128)(2,1)}, u32[]{:S(2)}) copy-start(bf16[1,6,1536]{2,1,0:T(8,128)(2,1)} %param.11) | copy-start | bytes 55300
  24.4 45.1 %collective-permute-start = (bf16[8,32,1152]{2,1,0:T(8,128)(2,1)S(1)}, bf16[8,32,1152]{2,1,0:T(8,128)(2,1)S(1)}, u32[]{:S(2)}, u32[]{:S(2)}) collective-permute-start(bf16[8,32,1152]{2,1,0:T(8,128)(2,1)S(1)} %get-tuple-element.15), channel_id=1, source_target_pairs={{0,16},{16,0},{1,17},{17,1},{2,18},{18,2},{3,19},{19,3},{4,20},{20... | collective-permute-start | bytes 1769480 | tf_op jit(solution)/shard_map/ppermute | solution.py:180
  39.3 3.1 %collective-permute-start.1 = (bf16[6,1536]{1,0:T(8,128)(2,1)S(1)}, bf16[6,1536]{1,0:T(8,128)(2,1)S(1)}, u32[]{:S(2)}, u32[]{:S(2)}) collective-permute-start(bf16[6,1536]{1,0:T(8,128)(2,1)S(1)} %bitcast.9), channel_id=1, source_target_pairs={{0,16},{16,0},{1,17},{17,1},{2,18},{18,2},{3,19},{19,3},{4,20},{20... | collective-permute-start | bytes 55304 | tf_op jit(solution)/shard_map/ppermute | solution.py:162
  42.4 25.6 %collective-permute-start.2 = (bf16[12,1536]{1,0:T(8,128)(2,1)S(1)}, bf16[12,1536]{1,0:T(8,128)(2,1)S(1)}, u32[]{:S(2)}, u32[]{:S(2)}) collective-permute-start(bf16[12,1536]{1,0:T(8,128)(2,1)S(1)} %pad_maximum_fusion.1), channel_id=1, source_target_pairs={{768,0},{802,2},{836,4},{870,6},{904,8},{938,10},{972,12},{1006,14... | collective-permute-start | bytes 110600 | tf_op jit(solution)/shard_map/ppermute | solution.py:165
  43.1 26.5 %collective-permute-start.3 = (bf16[12,1536]{1,0:T(8,128)(2,1)S(1)}, bf16[12,1536]{1,0:T(8,128)(2,1)S(1)}, u32[]{:S(2)}, u32[]{:S(2)}) collective-permute-start(bf16[12,1536]{1,0:T(8,128)(2,1)S(1)} %pad_maximum_fusion.1), channel_id=1, source_target_pairs={{256,0},{290,2},{324,4},{358,6},{392,8},{426,10},{460,12},{494,14}... | collective-permute-start | bytes 110600 | tf_op jit(solution)/shard_map/ppermute | solution.py:164
  98.9 18.9 %collective-permute-start.4 = (bf16[8,32,1152]{2,1,0:T(8,128)(2,1)S(1)}, bf16[8,32,1152]{2,1,0:T(8,128)(2,1)S(1)}, u32[]{:S(2)}, u32[]{:S(2)}) collective-permute-start(bf16[8,32,1152]{2,1,0:T(8,128)(2,1)S(1)} %get-tuple-element.16.here_ref), channel_id=1, source_target_pairs={{0,16},{16,0},{1,17},{17,1},{2,18},{18,2},{3,19},{19,3},{4,20},{20... | collective-permute-start | bytes 1769480 | tf_op jit(solution)/shard_map/ppermute | solution.py:206
  100.8 43.0 %all-to-all-start.2 = ((bf16[32,2,640]{2,1,0:T(2,128)(2,1)}), bf16[32,2,640]{2,1,0:T(2,128)(2,1)S(1)}, u32[]{:S(2)}, u32[]{:S(2)}) async-start(bf16[32,2,640]{2,1,0:T(2,128)(2,1)} %get-tuple-element.19), calls=%async_computation.2 | async-start | bytes 163840 | tf_op jit(solution)/shard_map/all_to_all | solution.py:203
  118.4 26.1 %collective-permute-start.5 = (bf16[64,1536]{1,0:T(8,128)(2,1)S(1)}, bf16[64,1536]{1,0:T(8,128)(2,1)S(1)}, u32[]{:S(2)}, u32[]{:S(2)}) collective-permute-start(bf16[64,1536]{1,0:T(8,128)(2,1)S(1)} %get-tuple-element.18), channel_id=1, source_target_pairs={{0,1},{1,0},{2,3},{3,2},{4,5},{5,4},{6,7},{7,6},{8,9},{9,8},{10,11... | collective-permute-start | bytes 589832 | tf_op jit(solution)/shard_map/ppermute | solution.py:214

commit v3 on v2

--- a/solution.py
+++ b/solution.py
@@ -13,7 +13,6 @@
 WIDTH = 1536
 HDM = 384
 CHUNK = 1152
-TAIL = WIDTH - CHUNK
 SEQ = ("yl", "x")
 F32 = jnp.float32
 BF16 = jnp.bfloat16
@@ -76,66 +75,66 @@
             ref[yl * 4 + 3] = rows[2][:, 384:]
 
 
-def merge_kernel(keep_ref, other_ref, near_ref, far_ref, out_ref):
-    rows = jnp.concatenate([near_ref[...].astype(F32), far_ref[...].astype(F32)], axis=0)
-    tails = [
-        jnp.concatenate([rows[3 * q + s : 3 * q + s + 1, CHUNK:] for s in range(3)], axis=1)
-        for q in range(8)
-    ]
-    block = jnp.concatenate([rows[:, :CHUNK]] + tails, axis=0).astype(BF16)
+def pair_kernel(k_ref, v_ref, out_ref, sems):
+    copies = []
     for j in range(SPANS):
-        out_ref[j, :ZS] = (keep_ref[j] + other_ref[j].astype(F32)).astype(BF16)
-        out_ref[j, ZS:] = block
+        for i, ref in enumerate((k_ref, v_ref)):
+            copies.append(
+                pltpu.make_async_copy(
+                    ref.at[0], out_ref.at[j, pl.ds(i * TOK, TOK), :], sems.at[2 * j + i]
+                )
+            )
+    for copy in copies:
+        copy.start()
+    for copy in copies:
+        copy.wait()
 
 
 def expand_kernel(att_ref, out_ref):
     core = lax.axis_index("c")
     depth = lax.axis_index("z")
+    x = lax.axis_index("x")
+    yl = lax.axis_index("yl")
     attended = att_ref[...]
-    p = lax.broadcasted_iota(jnp.int32, (1, 256), 1)
-    place, r = p // 32, p % 32
-    rows = lax.broadcasted_iota(jnp.int32, (HDM, 256), 0)
+    p = lax.broadcasted_iota(jnp.int32, (1, 192), 1)
+    place = (yl ^ ((p // 24) % 2)) * 4 + (x - p // 48 + 4) % 4
+    half, t = (p // 12) % 2, p % 12
+    rows = lax.broadcasted_iota(jnp.int32, (HDM, 192), 0)
     for part in range(2):
         side = part ^ core
-        for kind in range(4):
-            row = r if kind == 0 else 3 * (r - 24) + kind - 1
-            z = (depth + side * 8 + place - 8 + 16 * (row // 12) + ZS) % ZS
-            t = row % 12
-            feature = (z * 2 + ((t // 6) ^ side)) * 6 + t % 6
-            feature = jnp.where((r < 24) == (kind == 0), feature, -1)
-            pick = (rows == feature).astype(F32).astype(BF16)
-            out_ref[part, kind] = jnp.dot(attended, pick, preferred_element_type=F32).astype(BF16)
+        z = (depth + side * 8 + place - 8 + 16 * half + ZS) % ZS
+        feature = (z * 2 + ((t // 6) ^ side)) * 6 + t % 6
+        pick = (rows == feature).astype(F32).astype(BF16)
+        out_ref[part] = jnp.dot(attended, pick, preferred_element_type=F32).astype(BF16)
 
 
 def mix_kernel(wide_ref, here_ref, there_ref, own_ref, send_ref):
-    rank = lax.axis_index("yh")
-    head = jnp.zeros((TOK, CHUNK), F32)
-    tail = jnp.zeros((TOK, TAIL), F32)
-    for part, ref in ((0, here_ref), (1, there_ref)):
-        block = ref[...].reshape(256, CHUNK)
-        head = head + jnp.dot(wide_ref[part, 0], block, preferred_element_type=F32)
-        for s in range(3):
-            tail = tail + jnp.dot(
-                wide_ref[part, 1 + s],
-                block[:, s * TAIL : (s + 1) * TAIL],
-                preferred_element_type=F32,
-            )
-    first = rank == 0
-    for cols, m in ((slice(0, CHUNK), head), (slice(CHUNK, WIDTH), tail)):
-        own_ref[:, cols] = jnp.where(first, m[:64], m[64:])
-        send_ref[:, cols] = jnp.where(first, m[64:], m[:64]).astype(BF16)
-
-
-def fold_kernel(parts_ref, out_ref, here_ref):
-    total = parts_ref[0, :ZS].astype(F32)
+    mixed = jnp.dot(wide_ref[0], here_ref[...], preferred_element_type=F32)
+    mixed = mixed + jnp.dot(wide_ref[1], there_ref[...], preferred_element_type=F32)
+    first = lax.axis_index("yh") == 0
+    own_ref[...] = jnp.where(first, mixed[:64], mixed[64:])
+    send_ref[...] = jnp.where(first, mixed[64:], mixed[:64]).astype(BF16)
+
+
+def add_kernel(keep_ref, other_ref, out_ref):
+    out_ref[...] = (keep_ref[...] + other_ref[...].astype(F32)).astype(BF16)
+
+
+def fold_kernel(parts_ref, out_ref):
+    total = parts_ref[0].astype(F32)
     for j in range(1, SPANS):
-        total = total + parts_ref[j, :ZS].astype(F32)
+        total = total + parts_ref[j].astype(F32)
     total = total.astype(BF16)
     out_ref[:, 0, :] = total[:, :640]
     out_ref[:, 1, :512] = total[:, 640:]
     out_ref[:, 1, 512:] = jnp.zeros((ZS, 128), BF16)
-    for j in range(SPANS):
-        here_ref[j] = parts_ref[j, ZS:]
+
+
+def sum_kernel(parts_ref, out_ref):
+    total = jnp.sum(parts_ref[...].astype(F32), axis=0)
+    for j in range(9):
+        row, col = j // 5, (j % 5) * 128
+        out_ref[j] = total[row : row + 1, col : col + 128]
 
 
 def columns(shift):
@@ -155,8 +154,14 @@
 def local(queries, keys, values, proj_weight, gate_table, timestep, span_index, cotangent):
     S = jax.ShapeDtypeStruct
     swap = [(0, 1), (1, 0)]
-    pair = jnp.concatenate([keys[0], values[0]], axis=0)
-    pair = jnp.broadcast_to(pair[None], (SPANS,) + pair.shape)
+    pair = pl.pallas_call(
+        pair_kernel,
+        out_shape=S((SPANS, 2 * TOK, HDM), BF16),
+        in_specs=[VM, VM],
+        out_specs=pl.BlockSpec(memory_space=pl.ANY),
+        scratch_shapes=[pltpu.SemaphoreType.DMA((2 * SPANS,))],
+        compiler_params=vmem(4),
+    )(keys, values)
     pairs = lax.all_to_all(pair, SEQ, 0, 0, tiled=True)
     every = ("z", "c") + SEQ
     mate = lax.ppermute(proj_weight[0], "c", swap)
@@ -172,37 +177,53 @@
     )(timestep, cotangent, gate_table)
     keep, send, attended = pl.pallas_call(
         attend_kernel,
-        out_shape=(S((SPANS, ZS, CHUNK), F32), S((SPANS, ZS, CHUNK), BF16), S((TOK, HDM), BF16)),
+        out_shape=(
+            S((SPANS, ZS, CHUNK), F32),
+            S((SPANS, ZS, CHUNK), BF16),
+            S((TOK, HDM), BF16),
+        ),
         in_specs=[SM, VM, VM, VM],
         out_specs=(VM, VM, VM),
         compiler_params=vmem(20),
     )(span_index, queries, pairs, scaled)
     other = lax.ppermute(send, "c", swap)
+    dozens = jnp.concatenate([near, far], axis=0)
+    beside = lax.ppermute(dozens, "yl", swap)
+    block = jnp.concatenate([dozens, beside], axis=0)
     both = pl.pallas_call(
-        merge_kernel,
-        out_shape=S((SPANS, 2 * ZS, CHUNK), BF16),
-        in_specs=[VM, VM, VM, VM],
-        out_specs=VM,
-        compiler_params=vmem(8),
-    )(keep, other, near, far)
+        add_kernel,
+        out_shape=S((SPANS, ZS, CHUNK), BF16),
+        in_specs=[VM, VM],
+        out_specs=VM,
+        compiler_params=vmem(8),
+    )(keep, other)
     parts = lax.all_to_all(both, SEQ, 0, 0, tiled=True)
     wide = pl.pallas_call(
         expand_kernel,
-        out_shape=S((2, 4, TOK, 256), BF16),
+        out_shape=S((2, TOK, 192), BF16),
         in_specs=[VM],
         out_specs=VM,
         compiler_params=vmem(8),
     )(attended)
-    slices, here = pl.pallas_call(
+    blocks = [block]
+    for k in range(1, 4):
+        blocks.append(lax.ppermute(block, "x", [(i, (i + k) % 4) for i in range(4)]))
+    slices = pl.pallas_call(
         fold_kernel,
-        out_shape=(S((ZS, 2, 640), BF16), S((SPANS, ZS, CHUNK), BF16)),
+        out_shape=S((ZS, 2, 640), BF16),
         in_specs=[VM],
-        out_specs=(VM, VM),
+        out_specs=VM,
         compiler_params=vmem(8),
     )(parts)
     last = lax.all_to_all(slices, "z", 0, 0, tiled=True)
-    total = jnp.sum(last.astype(F32), axis=0).reshape(1280)[:CHUNK]
-    weight_grad = total.reshape(1, 9, 128)
+    weight_grad = pl.pallas_call(
+        sum_kernel,
+        out_shape=S((9, 1, 128), F32),
+        in_specs=[VM],
+        out_specs=VM,
+        compiler_params=vmem(8),
+    )(last).reshape(1, 9, 128)
+    here = jnp.concatenate(blocks, axis=0)
     there = lax.ppermute(here, "c", swap)
     own, away = pl.pallas_call(
         mix_kernel,

time: 146 us -> 141 us (0.966)
  the two profiles are of different devices: /device:TPU:1 before, /device:TPU:16 now
where the time goes in v3:
time: 141 us
  starting transfers between devices  79.9 us (57%)
  waiting for transfers between devices  47.9 us (34%)
  Pallas kernels  7.57 us (5%)
  local copies, waits for them, and re-layouts  2.2 us (2%)
  between operations  2.19 us (2%)
    all_to_all x1, waiting for transfers between devices, local(): last = lax.all_to_all(slices, 'z', 0, 0, tiled=True)  26.4 us
    all_to_all x1, starting transfers between devices, local(): last = lax.all_to_all(slices, 'z', 0, 0, tiled=True)  19.8 us
    ppermute x1, starting transfers between devices, local(): near = lax.ppermute(dozen, every, columns(0))  15.7 us
    ppermute x3, starting transfers between devices, local(): lax.ppermute(block, 'x', [(i, (i + k) % 4) for i in range(4)])  10.5 us
    ppermute x1, starting transfers between devices, local(): far = lax.ppermute(dozen, every, columns(16))  9.2 us
    all_to_all x1, waiting for transfers between devices, local(): parts = lax.all_to_all(both, SEQ, 0, 0, tiled=True)  8.24 us
    ppermute x1, starting transfers between devices, local(): other = lax.ppermute(send, 'c', swap)  6.5 us
    all_to_all x1, starting transfers between devices, local(): pairs = lax.all_to_all(pair, SEQ, 0, 0, tiled=True)  5.16 us
  transfers between devices with their start and end apart: 13, of which 7 were waited for; matrix products, arithmetic and copies ran while one was open for 1% of the time, Pallas kernels for 4%

profile of v3, /device:TPU:16, one launch (start us, length us, event | category | flops | bytes accessed | tf_op | source)
XLA Modules:
  0.0 140.6 jit_solution(9692227579195464449)
XLA Ops:
  0.6 0.0 copy-start.2
  0.6 0.9 copy-done.2
  1.5 0.0 copy-start.3
  1.5 0.9 copy-done.3
  2.4 1.3 shard_map.96
  3.7 0.0 copy-start.5
  3.7 0.0 copy-start
  3.8 0.0 copy-start.4
  3.8 0.0 copy-start.1
  3.8 5.2 %all-to-all-start = ((bf16[8,256,384]{2,1,0:T(8,128)(2,1)}), bf16[8,256,384]{2,1,0:T(8,128)(2,1)S(1)}, u32[]{:S(2)}, u32[]{:S(2)}) async-start(bf16[8,256,384]{2,1,0:T(8,128)(2,1)} %shard_map.96), calls=%async_computation | async-start | bytes 3145728 | tf_op jit(solution)/shard_map/all_to_all | solution.py:165
  8.9 0.0 copy-done.5
  8.9 1.9 %collective-permute-start = (bf16[6,1536]{1,0:T(8,128)(2,1)S(1)}, bf16[6,1536]{1,0:T(8,128)(2,1)S(1)}, u32[]{:S(2)}, u32[]{:S(2)}) collective-permute-start(bf16[6,1536]{1,0:T(8,128)(2,1)S(1)} %bitcast.4), channel_id=1, source_target_pairs={{0,16},{16,0},{1,17},{17,1},{2,18},{18,2},{3,19},{19,3},{4,20},{20... | collective-permute-start | bytes 55304 | tf_op jit(solution)/shard_map/ppermute | solution.py:167
  10.9 1.2 collective-permute-done
  12.1 15.7 %collective-permute-start.1 = (bf16[12,1536]{1,0:T(8,128)(2,1)S(1)}, bf16[12,1536]{1,0:T(8,128)(2,1)S(1)}, u32[]{:S(2)}, u32[]{:S(2)}) collective-permute-start(bf16[12,1536]{1,0:T(8,128)(2,1)S(1)} %pad_maximum_fusion.2), channel_id=1, source_target_pairs={{768,0},{802,2},{836,4},{870,6},{904,8},{938,10},{972,12},{1006,14... | collective-permute-start | bytes 110600 | tf_op jit(solution)/shard_map/ppermute | solution.py:170
  27.8 9.2 %collective-permute-start.2 = (bf16[12,1536]{1,0:T(8,128)(2,1)S(1)}, bf16[12,1536]{1,0:T(8,128)(2,1)S(1)}, u32[]{:S(2)}, u32[]{:S(2)}) collective-permute-start(bf16[12,1536]{1,0:T(8,128)(2,1)S(1)} %pad_maximum_fusion.2), channel_id=1, source_target_pairs={{256,0},{290,2},{324,4},{358,6},{392,8},{426,10},{460,12},{494,14}... | collective-permute-start | bytes 110600 | tf_op jit(solution)/shard_map/ppermute | solution.py:169
  38.3 0.0 copy-done
  38.3 0.0 copy-done.4
  38.3 0.1 shard_map.95
  38.4 0.0 all-to-all-done.kv_ref
  38.4 0.0 copy-done.1
  38.4 3.2 %shard_map.97 = (f32[8,32,1152]{2,1,0:T(8,128)S(1)}, bf16[8,32,1152]{2,1,0:T(8,128)(2,1)}, bf16[128,384]{1,0:T(8,128)(2,1)S(1)}) custom-call(s32[1]{0:T(128)S(6)} %copy.11.si_ref, bf16[1,128,384]{2,1,0:T(8,128)(2,1)S(1)} %copy-done.1, bf16[8,256,384]{2,1,0:T(8,128)(2,1)S(1)} %all-to-all-done.kv_ref, bf16[128,1536]{1,0:T(8,128)(2,1)S(1)} %get-tuple-element.10.scaled_ref), custom_call_target="tpu_custom_call" | custom-call | tf_op jit(solution)/shard_map/pallas_call | solution.py:178
  41.6 6.5 %collective-permute-start.9 = (bf16[8,32,1152]{2,1,0:T(8,128)(2,1)}, bf16[8,32,1152]{2,1,0:T(8,128)(2,1)S(1)}, u32[]{:S(2)}, u32[]{:S(2)}) collective-permute-start(bf16[8,32,1152]{2,1,0:T(8,128)(2,1)} %get-tuple-element.15), channel_id=1, source_target_pairs={{0,16},{16,0},{1,17},{17,1},{2,18},{18,2},{3,19},{19,3},{4,20},{20... | collective-permute-start | bytes 1769480 | tf_op jit(solution)/shard_map/ppermute | solution.py:189
  48.1 0.0 collective-permute-done.1
  48.1 2.8 %collective-permute-done.2 = bf16[12,1536]{1,0:T(8,128)(2,1)S(1)} collective-permute-done((bf16[12,1536]{1,0:T(8,128)(2,1)S(1)}, bf16[12,1536]{1,0:T(8,128)(2,1)S(1)}, u32[]{:S(2)}, u32[]{:S(2)}) %collective-permute-start.2) | collective-permute-done | bytes 36896 | tf_op jit(solution)/shard_map/ppermute | solution.py:169
  50.9 1.9 %collective-permute-start.3 = (bf16[24,1536]{1,0:T(8,128)(2,1)S(1)}, bf16[24,1536]{1,0:T(8,128)(2,1)S(1)}, u32[]{:S(2)}, u32[]{:S(2)}) collective-permute-start(bf16[24,1536]{1,0:T(8,128)(2,1)S(1)} %pad_maximum_fusion.1), channel_id=1, source_target_pairs={{0,8},{8,0},{1,9},{9,1},{2,10},{10,2},{3,11},{11,3},{4,12},{12,4},... | collective-permute-start | bytes 221192 | tf_op jit(solution)/shard_map/ppermute | solution.py:191
  52.9 4.3 %collective-permute-done.3 = bf16[24,1536]{1,0:T(8,128)(2,1)S(1)} collective-permute-done((bf16[24,1536]{1,0:T(8,128)(2,1)S(1)}, bf16[24,1536]{1,0:T(8,128)(2,1)S(1)}, u32[]{:S(2)}, u32[]{:S(2)}) %collective-permute-start.3) | collective-permute-done | bytes 73760 | tf_op jit(solution)/shard_map/ppermute | solution.py:191
  57.2 3.7 %collective-permute-start.4 = (bf16[48,1536]{1,0:T(8,128)(2,1)S(1)}, bf16[48,1536]{1,0:T(8,128)(2,1)S(1)}, u32[]{:S(2)}, u32[]{:S(2)}) collective-permute-start(bf16[48,1536]{1,0:T(8,128)(2,1)S(1)} %pad_maximum_fusion), channel_id=1, source_target_pairs={{0,2},{2,4},{4,6},{6,0},{1,3},{3,5},{5,7},{7,1},{8,10},{10,12},{12... | collective-permute-start | bytes 442376 | tf_op jit(solution)/shard_map/ppermute | solution.py:210
  60.9 3.5 %collective-permute-start.5 = (bf16[48,1536]{1,0:T(8,128)(2,1)S(1)}, bf16[48,1536]{1,0:T(8,128)(2,1)S(1)}, u32[]{:S(2)}, u32[]{:S(2)}) collective-permute-start(bf16[48,1536]{1,0:T(8,128)(2,1)S(1)} %pad_maximum_fusion), channel_id=1, source_target_pairs={{0,4},{2,6},{4,0},{6,2},{1,5},{3,7},{5,1},{7,3},{8,12},{10,14},{12... | collective-permute-start | bytes 442376 | tf_op jit(solution)/shard_map/ppermute | solution.py:210
  64.4 3.3 %collective-permute-start.6 = (bf16[48,1536]{1,0:T(8,128)(2,1)S(1)}, bf16[48,1536]{1,0:T(8,128)(2,1)S(1)}, u32[]{:S(2)}, u32[]{:S(2)}) collective-permute-start(bf16[48,1536]{1,0:T(8,128)(2,1)S(1)} %pad_maximum_fusion), channel_id=1, source_target_pairs={{0,6},{2,0},{4,2},{6,4},{1,7},{3,1},{5,3},{7,5},{8,14},{10,8},{12,... | collective-permute-start | bytes 442376 | tf_op jit(solution)/shard_map/ppermute | solution.py:210
  67.7 0.0 collective-permute-done.4
  67.8 3.1 %collective-permute-done.5 = bf16[48,1536]{1,0:T(8,128)(2,1)S(1)} collective-permute-done((bf16[48,1536]{1,0:T(8,128)(2,1)S(1)}, bf16[48,1536]{1,0:T(8,128)(2,1)S(1)}, u32[]{:S(2)}, u32[]{:S(2)}) %collective-permute-start.5) | collective-permute-done | bytes 147488 | tf_op jit(solution)/shard_map/ppermute | solution.py:210
  70.8 1.9 %collective-permute-done.6 = bf16[48,1536]{1,0:T(8,128)(2,1)S(1)} collective-permute-done((bf16[48,1536]{1,0:T(8,128)(2,1)S(1)}, bf16[48,1536]{1,0:T(8,128)(2,1)S(1)}, u32[]{:S(2)}, u32[]{:S(2)}) %collective-permute-start.6) | collective-permute-done | bytes 147488 | tf_op jit(solution)/shard_map/ppermute | solution.py:210
  72.7 0.4 concatenate.17.here_ref
  73.2 1.9 %collective-permute-start.7 = (bf16[192,1536]{1,0:T(8,128)(2,1)S(1)}, bf16[192,1536]{1,0:T(8,128)(2,1)S(1)}, u32[]{:S(2)}, u32[]{:S(2)}) collective-permute-start(bf16[192,1536]{1,0:T(8,128)(2,1)S(1)} %concatenate.17.here_ref), channel_id=1, source_target_pairs={{0,16},{16,0},{1,17},{17,1},{2,18},{18,2},{3,19},{19,3},{4,20},{20... | collective-permute-start | bytes 1769480 | tf_op jit(solution)/shard_map/ppermute | solution.py:227
  75.1 0.0 collective-permute-done.9.other_ref
  75.1 0.9 shard_map.100
  76.0 4.7 %all-to-all-start.1 = ((bf16[8,32,1152]{2,1,0:T(8,128)(2,1)}), bf16[8,32,1152]{2,1,0:T(8,128)(2,1)S(1)}, u32[]{:S(2)}, u32[]{:S(2)}) async-start(bf16[8,32,1152]{2,1,0:T(8,128)(2,1)} %shard_map.100), calls=%async_computation.1 | async-start | bytes 1179648 | tf_op jit(solution)/shard_map/all_to_all | solution.py:200
  80.7 0.3 shard_map.98.wide_ref
  81.0 0.0 collective-permute-done.7.there_ref
  81.0 0.4 shard_map.99
  81.4 2.5 %collective-permute-start.8 = (bf16[64,1536]{1,0:T(8,128)(2,1)S(1)}, bf16[64,1536]{1,0:T(8,128)(2,1)S(1)}, u32[]{:S(2)}, u32[]{:S(2)}) collective-permute-start(bf16[64,1536]{1,0:T(8,128)(2,1)S(1)} %get-tuple-element.13), channel_id=1, source_target_pairs={{0,1},{1,0},{2,3},{3,2},{4,5},{5,4},{6,7},{7,6},{8,9},{9,8},{10,11... | collective-permute-start | bytes 589832 | tf_op jit(solution)/shard_map/ppermute | solution.py:235
  83.9 8.2 %all-to-all-done.1.parts_ref = bf16[8,32,1152]{2,1,0:T(8,128)(2,1)S(1)} async-done(((bf16[8,32,1152]{2,1,0:T(8,128)(2,1)}), bf16[8,32,1152]{2,1,0:T(8,128)(2,1)S(1)}, u32[]{:S(2)}, u32[]{:S(2)}) %all-to-all-start.1) | async-done | bytes 589856 | tf_op jit(solution)/shard_map/all_to_all | solution.py:200
  92.2 0.8 shard_map.101
  92.9 19.8 %all-to-all-start.2 = ((bf16[32,2,640]{2,1,0:T(2,128)(2,1)}), bf16[32,2,640]{2,1,0:T(2,128)(2,1)S(1)}, u32[]{:S(2)}, u32[]{:S(2)}) async-start(bf16[32,2,640]{2,1,0:T(2,128)(2,1)} %shard_map.101), calls=%async_computation.2 | async-start | bytes 163840 | tf_op jit(solution)/shard_map/all_to_all | solution.py:218
  112.7 0.0 collective-permute-done.8
  112.7 0.7 fusion
  113.5 26.4 %all-to-all-done.2.parts_ref = bf16[32,2,640]{2,1,0:T(2,128)(2,1)S(1)} async-done(((bf16[32,2,640]{2,1,0:T(2,128)(2,1)}), bf16[32,2,640]{2,1,0:T(2,128)(2,1)S(1)}, u32[]{:S(2)}, u32[]{:S(2)}) %all-to-all-start.2) | async-done | bytes 81952 | tf_op jit(solution)/shard_map/all_to_all | solution.py:218
  139.9 0.7 shard_map.102
  (4 shorter events, 0.1 us)
Async XLA Ops:
  0.6 0.9 copy-start.2
  1.5 0.9 copy-start.3
  3.7 5.2 %copy-start.5 = (bf16[1,6,1536]{2,1,0:T(8,128)(2,1)S(1)}, bf16[1,6,1536]{2,1,0:T(8,128)(2,1)}, u32[]{:S(2)}) copy-start(bf16[1,6,1536]{2,1,0:T(8,128)(2,1)} %param.11) | copy-start | bytes 55300
  3.7 34.6 %copy-start = (bf16[1,128,1536]{2,1,0:T(8,128)(2,1)S(1)}, bf16[1,128,1536]{2,1,0:T(8,128)(2,1)}, u32[]{:S(2)}) copy-start(bf16[1,128,1536]{2,1,0:T(8,128)(2,1)} %cot_ref.1) | copy-start | bytes 1179652
  3.8 34.5 %copy-start.4 = (f32[4,1536]{1,0:T(4,128)S(1)}, f32[4,1536]{1,0:T(4,128)}, u32[]{:S(2)}) copy-start(f32[4,1536]{1,0:T(4,128)} %table_ref.1) | copy-start | bytes 73732
  3.8 34.6 %copy-start.1 = (bf16[1,128,384]{2,1,0:T(8,128)(2,1)S(1)}, bf16[1,128,384]{2,1,0:T(8,128)(2,1)}, u32[]{:S(2)}) copy-start(bf16[1,128,384]{2,1,0:T(8,128)(2,1)} %q_ref.1) | copy-start | bytes 294916
  3.8 34.6 %all-to-all-start = ((bf16[8,256,384]{2,1,0:T(8,128)(2,1)}), bf16[8,256,384]{2,1,0:T(8,128)(2,1)S(1)}, u32[]{:S(2)}, u32[]{:S(2)}) async-start(bf16[8,256,384]{2,1,0:T(8,128)(2,1)} %shard_map.96), calls=%async_computation | async-start | bytes 3145728 | tf_op jit(solution)/shard_map/all_to_all | solution.py:165
  8.9 3.1 %collective-permute-start = (bf16[6,1536]{1,0:T(8,128)(2,1)S(1)}, bf16[6,1536]{1,0:T(8,128)(2,1)S(1)}, u32[]{:S(2)}, u32[]{:S(2)}) collective-permute-start(bf16[6,1536]{1,0:T(8,128)(2,1)S(1)} %bitcast.4), channel_id=1, source_target_pairs={{0,16},{16,0},{1,17},{17,1},{2,18},{18,2},{3,19},{19,3},{4,20},{20... | collective-permute-start | bytes 55304 | tf_op jit(solution)/shard_map/ppermute | solution.py:167
  12.1 36.1 %collective-permute-start.1 = (bf16[12,1536]{1,0:T(8,128)(2,1)S(1)}, bf16[12,1536]{1,0:T(8,128)(2,1)S(1)}, u32[]{:S(2)}, u32[]{:S(2)}) collective-permute-start(bf16[12,1536]{1,0:T(8,128)(2,1)S(1)} %pad_maximum_fusion.2), channel_id=1, source_target_pairs={{768,0},{802,2},{836,4},{870,6},{904,8},{938,10},{972,12},{1006,14... | collective-permute-start | bytes 110600 | tf_op jit(solution)/shard_map/ppermute | solution.py:170
  27.8 23.1 %collective-permute-start.2 = (bf16[12,1536]{1,0:T(8,128)(2,1)S(1)}, bf16[12,1536]{1,0:T(8,128)(2,1)S(1)}, u32[]{:S(2)}, u32[]{:S(2)}) collective-permute-start(bf16[12,1536]{1,0:T(8,128)(2,1)S(1)} %pad_maximum_fusion.2), channel_id=1, source_target_pairs={{256,0},{290,2},{324,4},{358,6},{392,8},{426,10},{460,12},{494,14}... | collective-permute-start | bytes 110600 | tf_op jit(solution)/shard_map/ppermute | solution.py:169
  41.6 33.5 %collective-permute-start.9 = (bf16[8,32,1152]{2,1,0:T(8,128)(2,1)}, bf16[8,32,1152]{2,1,0:T(8,128)(2,1)S(1)}, u32[]{:S(2)}, u32[]{:S(2)}) collective-permute-start(bf16[8,32,1152]{2,1,0:T(8,128)(2,1)} %get-tuple-element.15), channel_id=1, source_target_pairs={{0,16},{16,0},{1,17},{17,1},{2,18},{18,2},{3,19},{19,3},{4,20},{20... | collective-permute-start | bytes 1769480 | tf_op jit(solution)/shard_map/ppermute | solution.py:189
  50.9 6.2 %collective-permute-start.3 = (bf16[24,1536]{1,0:T(8,128)(2,1)S(1)}, bf16[24,1536]{1,0:T(8,128)(2,1)S(1)}, u32[]{:S(2)}, u32[]{:S(2)}) collective-permute-start(bf16[24,1536]{1,0:T(8,128)(2,1)S(1)} %pad_maximum_fusion.1), channel_id=1, source_target_pairs={{0,8},{8,0},{1,9},{9,1},{2,10},{10,2},{3,11},{11,3},{4,12},{12,4},... | collective-permute-start | bytes 221192 | tf_op jit(solution)/shard_map/ppermute | solution.py:191
  57.2 10.5 %collective-permute-start.4 = (bf16[48,1536]{1,0:T(8,128)(2,1)S(1)}, bf16[48,1536]{1,0:T(8,128)(2,1)S(1)}, u32[]{:S(2)}, u32[]{:S(2)}) collective-permute-start(bf16[48,1536]{1,0:T(8,128)(2,1)S(1)} %pad_maximum_fusion), channel_id=1, source_target_pairs={{0,2},{2,4},{4,6},{6,0},{1,3},{3,5},{5,7},{7,1},{8,10},{10,12},{12... | collective-permute-start | bytes 442376 | tf_op jit(solution)/shard_map/ppermute | solution.py:210
  60.9 10.0 %collective-permute-start.5 = (bf16[48,1536]{1,0:T(8,128)(2,1)S(1)}, bf16[48,1536]{1,0:T(8,128)(2,1)S(1)}, u32[]{:S(2)}, u32[]{:S(2)}) collective-permute-start(bf16[48,1536]{1,0:T(8,128)(2,1)S(1)} %pad_maximum_fusion), channel_id=1, source_target_pairs={{0,4},{2,6},{4,0},{6,2},{1,5},{3,7},{5,1},{7,3},{8,12},{10,14},{12... | collective-permute-start | bytes 442376 | tf_op jit(solution)/shard_map/ppermute | solution.py:210
  64.4 8.3 %collective-permute-start.6 = (bf16[48,1536]{1,0:T(8,128)(2,1)S(1)}, bf16[48,1536]{1,0:T(8,128)(2,1)S(1)}, u32[]{:S(2)}, u32[]{:S(2)}) collective-permute-start(bf16[48,1536]{1,0:T(8,128)(2,1)S(1)} %pad_maximum_fusion), channel_id=1, source_target_pairs={{0,6},{2,0},{4,2},{6,4},{1,7},{3,1},{5,3},{7,5},{8,14},{10,8},{12,... | collective-permute-start | bytes 442376 | tf_op jit(solution)/shard_map/ppermute | solution.py:210
  73.2 7.9 %collective-permute-start.7 = (bf16[192,1536]{1,0:T(8,128)(2,1)S(1)}, bf16[192,1536]{1,0:T(8,128)(2,1)S(1)}, u32[]{:S(2)}, u32[]{:S(2)}) collective-permute-start(bf16[192,1536]{1,0:T(8,128)(2,1)S(1)} %concatenate.17.here_ref), channel_id=1, source_target_pairs={{0,16},{16,0},{1,17},{17,1},{2,18},{18,2},{3,19},{19,3},{4,20},{20... | collective-permute-start | bytes 1769480 | tf_op jit(solution)/shard_map/ppermute | solution.py:227
  76.0 16.2 %all-to-all-start.1 = ((bf16[8,32,1152]{2,1,0:T(8,128)(2,1)}), bf16[8,32,1152]{2,1,0:T(8,128)(2,1)S(1)}, u32[]{:S(2)}, u32[]{:S(2)}) async-start(bf16[8,32,1152]{2,1,0:T(8,128)(2,1)} %shard_map.100), calls=%async_computation.1 | async-start | bytes 1179648 | tf_op jit(solution)/shard_map/all_to_all | solution.py:200
  81.4 31.4 %collective-permute-start.8 = (bf16[64,1536]{1,0:T(8,128)(2,1)S(1)}, bf16[64,1536]{1,0:T(8,128)(2,1)S(1)}, u32[]{:S(2)}, u32[]{:S(2)}) collective-permute-start(bf16[64,1536]{1,0:T(8,128)(2,1)S(1)} %get-tuple-element.13), channel_id=1, source_target_pairs={{0,1},{1,0},{2,3},{3,2},{4,5},{5,4},{6,7},{7,6},{8,9},{9,8},{10,11... | collective-permute-start | bytes 589832 | tf_op jit(solution)/shard_map/ppermute | solution.py:235
  92.9 46.9 %all-to-all-start.2 = ((bf16[32,2,640]{2,1,0:T(2,128)(2,1)}), bf16[32,2,640]{2,1,0:T(2,128)(2,1)S(1)}, u32[]{:S(2)}, u32[]{:S(2)}) async-start(bf16[32,2,640]{2,1,0:T(2,128)(2,1)} %shard_map.101), calls=%async_computation.2 | async-start | bytes 163840 | tf_op jit(solution)/shard_map/all_to_all | solution.py:218

commit v4 on v3

--- a/solution.py
+++ b/solution.py
@@ -75,17 +75,22 @@
             ref[yl * 4 + 3] = rows[2][:, 384:]
 
 
-def pair_kernel(k_ref, v_ref, out_ref, sems):
+def pair_kernel(k_ref, v_ref, out_ref, held, in_sems, sems):
+    loads = [
+        pltpu.make_async_copy(ref.at[0], held.at[i], in_sems.at[i])
+        for i, ref in enumerate((k_ref, v_ref))
+    ]
+    for load in loads:
+        load.start()
     copies = []
-    for j in range(SPANS):
-        for i, ref in enumerate((k_ref, v_ref)):
-            copies.append(
-                pltpu.make_async_copy(
-                    ref.at[0], out_ref.at[j, pl.ds(i * TOK, TOK), :], sems.at[2 * j + i]
-                )
+    for i, load in enumerate(loads):
+        load.wait()
+        for j in range(SPANS):
+            copy = pltpu.make_async_copy(
+                held.at[i], out_ref.at[j, pl.ds(i * TOK, TOK), :], sems.at[i * SPANS + j]
             )
-    for copy in copies:
-        copy.start()
+            copy.start()
+            copies.append(copy)
     for copy in copies:
         copy.wait()
 
@@ -157,10 +162,14 @@
     pair = pl.pallas_call(
         pair_kernel,
         out_shape=S((SPANS, 2 * TOK, HDM), BF16),
-        in_specs=[VM, VM],
+        in_specs=[pl.BlockSpec(memory_space=pltpu.HBM)] * 2,
         out_specs=pl.BlockSpec(memory_space=pl.ANY),
-        scratch_shapes=[pltpu.SemaphoreType.DMA((2 * SPANS,))],
-        compiler_params=vmem(4),
+        scratch_shapes=[
+            pltpu.VMEM((2, TOK, HDM), BF16),
+            pltpu.SemaphoreType.DMA((2,)),
+            pltpu.SemaphoreType.DMA((2 * SPANS,)),
+        ],
+        compiler_params=pltpu.CompilerParams(vmem_limit_bytes=67043328),
     )(keys, values)
     pairs = lax.all_to_all(pair, SEQ, 0, 0, tiled=True)
     every = ("z", "c") + SEQ

time: 141 us -> 140 us (level)
  local copies, waits for them, and re-layouts: 2.2 us -> 0.43 us
    unnamed x12 -> x8, local copies, waits for them, and re-layouts: 1.8 us -> 0.03 us
where the time goes in v4:
time: 140 us
  starting transfers between devices  79.9 us (57%)
  waiting for transfers between devices  47.9 us (34%)
  Pallas kernels  8.53 us (6%)
  between operations  2.18 us (2%)
    all_to_all x1, waiting for transfers between devices, local(): last = lax.all_to_all(slices, 'z', 0, 0, tiled=True)  26.4 us
    all_to_all x1, starting transfers between devices, local(): last = lax.all_to_all(slices, 'z', 0, 0, tiled=True)  19.7 us
    ppermute x1, starting transfers between devices, local(): near = lax.ppermute(dozen, every, columns(0))  15.7 us
    ppermute x3, starting transfers between devices, local(): lax.ppermute(block, 'x', [(i, (i + k) % 4) for i in range(4)])  10.5 us
    ppermute x1, starting transfers between devices, local(): far = lax.ppermute(dozen, every, columns(16))  9.2 us
    all_to_all x1, waiting for transfers between devices, local(): parts = lax.all_to_all(both, SEQ, 0, 0, tiled=True)  8.23 us
    ppermute x1, starting transfers between devices, local(): other = lax.ppermute(send, 'c', swap)  6.5 us
    all_to_all x1, starting transfers between devices, local(): pairs = lax.all_to_all(pair, SEQ, 0, 0, tiled=True)  5.16 us
  transfers between devices with their start and end apart: 13, of which 7 were waited for; matrix products, arithmetic and copies ran while one was open for 1% of the time, Pallas kernels for 4%

profile of v4, /device:TPU:16, one launch (start us, length us, event | category | flops | bytes accessed | tf_op | source)
XLA Modules:
  0.0 139.7 jit_solution(7803779094525171340)
XLA Ops:
  0.6 2.2 %shard_map.96 = bf16[8,256,384]{2,1,0:T(8,128)(2,1)} custom-call(bf16[1,128,384]{2,1,0:T(8,128)(2,1)} %k_ref.1, bf16[1,128,384]{2,1,0:T(8,128)(2,1)} %v_ref.1), custom_call_target="tpu_custom_call" | custom-call | tf_op jit(solution)/shard_map/pallas_call | solution.py:162
  2.9 0.0 copy-start.3
  2.9 0.0 copy-start
  2.9 0.0 copy-start.2
  2.9 0.0 copy-start.1
  2.9 5.2 %all-to-all-start = ((bf16[8,256,384]{2,1,0:T(8,128)(2,1)}), bf16[8,256,384]{2,1,0:T(8,128)(2,1)S(1)}, u32[]{:S(2)}, u32[]{:S(2)}) async-start(bf16[8,256,384]{2,1,0:T(8,128)(2,1)} %shard_map.96), calls=%async_computation | async-start | bytes 3145728 | tf_op jit(solution)/shard_map/all_to_all | solution.py:174
  8.1 0.0 copy-done.3
  8.1 1.9 %collective-permute-start = (bf16[6,1536]{1,0:T(8,128)(2,1)S(1)}, bf16[6,1536]{1,0:T(8,128)(2,1)S(1)}, u32[]{:S(2)}, u32[]{:S(2)}) collective-permute-start(bf16[6,1536]{1,0:T(8,128)(2,1)S(1)} %bitcast.4), channel_id=1, source_target_pairs={{0,16},{16,0},{1,17},{17,1},{2,18},{18,2},{3,19},{19,3},{4,20},{20... | collective-permute-start | bytes 55304 | tf_op jit(solution)/shard_map/ppermute | solution.py:176
  10.0 1.2 collective-permute-done
  11.2 15.7 %collective-permute-start.1 = (bf16[12,1536]{1,0:T(8,128)(2,1)S(1)}, bf16[12,1536]{1,0:T(8,128)(2,1)S(1)}, u32[]{:S(2)}, u32[]{:S(2)}) collective-permute-start(bf16[12,1536]{1,0:T(8,128)(2,1)S(1)} %pad_maximum_fusion.2), channel_id=1, source_target_pairs={{768,0},{802,2},{836,4},{870,6},{904,8},{938,10},{972,12},{1006,14... | collective-permute-start | bytes 110600 | tf_op jit(solution)/shard_map/ppermute | solution.py:179
  26.9 9.2 %collective-permute-start.2 = (bf16[12,1536]{1,0:T(8,128)(2,1)S(1)}, bf16[12,1536]{1,0:T(8,128)(2,1)S(1)}, u32[]{:S(2)}, u32[]{:S(2)}) collective-permute-start(bf16[12,1536]{1,0:T(8,128)(2,1)S(1)} %pad_maximum_fusion.2), channel_id=1, source_target_pairs={{256,0},{290,2},{324,4},{358,6},{392,8},{426,10},{460,12},{494,14}... | collective-permute-start | bytes 110600 | tf_op jit(solution)/shard_map/ppermute | solution.py:178
  37.4 0.0 copy-done
  37.4 0.0 copy-done.2
  37.4 0.1 shard_map.95
  37.5 0.0 all-to-all-done.kv_ref
  37.5 0.0 copy-done.1
  37.5 3.2 %shard_map.97 = (f32[8,32,1152]{2,1,0:T(8,128)S(1)}, bf16[8,32,1152]{2,1,0:T(8,128)(2,1)}, bf16[128,384]{1,0:T(8,128)(2,1)S(1)}) custom-call(s32[1]{0:T(128)S(6)} %copy.11.si_ref, bf16[1,128,384]{2,1,0:T(8,128)(2,1)S(1)} %copy-done.1, bf16[8,256,384]{2,1,0:T(8,128)(2,1)S(1)} %all-to-all-done.kv_ref, bf16[128,1536]{1,0:T(8,128)(2,1)S(1)} %get-tuple-element.10.scaled_ref), custom_call_target="tpu_custom_call" | custom-call | tf_op jit(solution)/shard_map/pallas_call | solution.py:187
  40.8 6.5 %collective-permute-start.9 = (bf16[8,32,1152]{2,1,0:T(8,128)(2,1)}, bf16[8,32,1152]{2,1,0:T(8,128)(2,1)S(1)}, u32[]{:S(2)}, u32[]{:S(2)}) collective-permute-start(bf16[8,32,1152]{2,1,0:T(8,128)(2,1)} %get-tuple-element.15), channel_id=1, source_target_pairs={{0,16},{16,0},{1,17},{17,1},{2,18},{18,2},{3,19},{19,3},{4,20},{20... | collective-permute-start | bytes 1769480 | tf_op jit(solution)/shard_map/ppermute | solution.py:198
  47.3 0.0 collective-permute-done.1
  47.3 2.8 %collective-permute-done.2 = bf16[12,1536]{1,0:T(8,128)(2,1)S(1)} collective-permute-done((bf16[12,1536]{1,0:T(8,128)(2,1)S(1)}, bf16[12,1536]{1,0:T(8,128)(2,1)S(1)}, u32[]{:S(2)}, u32[]{:S(2)}) %collective-permute-start.2) | collective-permute-done | bytes 36896 | tf_op jit(solution)/shard_map/ppermute | solution.py:178
  50.1 1.9 %collective-permute-start.3 = (bf16[24,1536]{1,0:T(8,128)(2,1)S(1)}, bf16[24,1536]{1,0:T(8,128)(2,1)S(1)}, u32[]{:S(2)}, u32[]{:S(2)}) collective-permute-start(bf16[24,1536]{1,0:T(8,128)(2,1)S(1)} %pad_maximum_fusion.1), channel_id=1, source_target_pairs={{0,8},{8,0},{1,9},{9,1},{2,10},{10,2},{3,11},{11,3},{4,12},{12,4},... | collective-permute-start | bytes 221192 | tf_op jit(solution)/shard_map/ppermute | solution.py:200
  52.0 4.3 %collective-permute-done.3 = bf16[24,1536]{1,0:T(8,128)(2,1)S(1)} collective-permute-done((bf16[24,1536]{1,0:T(8,128)(2,1)S(1)}, bf16[24,1536]{1,0:T(8,128)(2,1)S(1)}, u32[]{:S(2)}, u32[]{:S(2)}) %collective-permute-start.3) | collective-permute-done | bytes 73760 | tf_op jit(solution)/shard_map/ppermute | solution.py:200
  56.4 3.7 %collective-permute-start.4 = (bf16[48,1536]{1,0:T(8,128)(2,1)S(1)}, bf16[48,1536]{1,0:T(8,128)(2,1)S(1)}, u32[]{:S(2)}, u32[]{:S(2)}) collective-permute-start(bf16[48,1536]{1,0:T(8,128)(2,1)S(1)} %pad_maximum_fusion), channel_id=1, source_target_pairs={{0,2},{2,4},{4,6},{6,0},{1,3},{3,5},{5,7},{7,1},{8,10},{10,12},{12... | collective-permute-start | bytes 442376 | tf_op jit(solution)/shard_map/ppermute | solution.py:219
  60.0 3.5 %collective-permute-start.5 = (bf16[48,1536]{1,0:T(8,128)(2,1)S(1)}, bf16[48,1536]{1,0:T(8,128)(2,1)S(1)}, u32[]{:S(2)}, u32[]{:S(2)}) collective-permute-start(bf16[48,1536]{1,0:T(8,128)(2,1)S(1)} %pad_maximum_fusion), channel_id=1, source_target_pairs={{0,4},{2,6},{4,0},{6,2},{1,5},{3,7},{5,1},{7,3},{8,12},{10,14},{12... | collective-permute-start | bytes 442376 | tf_op jit(solution)/shard_map/ppermute | solution.py:219
  63.6 3.3 %collective-permute-start.6 = (bf16[48,1536]{1,0:T(8,128)(2,1)S(1)}, bf16[48,1536]{1,0:T(8,128)(2,1)S(1)}, u32[]{:S(2)}, u32[]{:S(2)}) collective-permute-start(bf16[48,1536]{1,0:T(8,128)(2,1)S(1)} %pad_maximum_fusion), channel_id=1, source_target_pairs={{0,6},{2,0},{4,2},{6,4},{1,7},{3,1},{5,3},{7,5},{8,14},{10,8},{12,... | collective-permute-start | bytes 442376 | tf_op jit(solution)/shard_map/ppermute | solution.py:219
  66.9 0.0 collective-permute-done.4
  66.9 3.1 %collective-permute-done.5 = bf16[48,1536]{1,0:T(8,128)(2,1)S(1)} collective-permute-done((bf16[48,1536]{1,0:T(8,128)(2,1)S(1)}, bf16[48,1536]{1,0:T(8,128)(2,1)S(1)}, u32[]{:S(2)}, u32[]{:S(2)}) %collective-permute-start.5) | collective-permute-done | bytes 147488 | tf_op jit(solution)/shard_map/ppermute | solution.py:219
  70.0 1.9 %collective-permute-done.6 = bf16[48,1536]{1,0:T(8,128)(2,1)S(1)} collective-permute-done((bf16[48,1536]{1,0:T(8,128)(2,1)S(1)}, bf16[48,1536]{1,0:T(8,128)(2,1)S(1)}, u32[]{:S(2)}, u32[]{:S(2)}) %collective-permute-start.6) | collective-permute-done | bytes 147488 | tf_op jit(solution)/shard_map/ppermute | solution.py:219
  71.9 0.4 concatenate.17.here_ref
  72.3 1.9 %collective-permute-start.7 = (bf16[192,1536]{1,0:T(8,128)(2,1)S(1)}, bf16[192,1536]{1,0:T(8,128)(2,1)S(1)}, u32[]{:S(2)}, u32[]{:S(2)}) collective-permute-start(bf16[192,1536]{1,0:T(8,128)(2,1)S(1)} %concatenate.17.here_ref), channel_id=1, source_target_pairs={{0,16},{16,0},{1,17},{17,1},{2,18},{18,2},{3,19},{19,3},{4,20},{20... | collective-permute-start | bytes 1769480 | tf_op jit(solution)/shard_map/ppermute | solution.py:236
  74.2 0.0 collective-permute-done.9.other_ref
  74.2 0.9 shard_map.100
  75.2 4.7 %all-to-all-start.1 = ((bf16[8,32,1152]{2,1,0:T(8,128)(2,1)}), bf16[8,32,1152]{2,1,0:T(8,128)(2,1)S(1)}, u32[]{:S(2)}, u32[]{:S(2)}) async-start(bf16[8,32,1152]{2,1,0:T(8,128)(2,1)} %shard_map.100), calls=%async_computation.1 | async-start | bytes 1179648 | tf_op jit(solution)/shard_map/all_to_all | solution.py:209
  79.9 0.3 shard_map.98.wide_ref
  80.2 0.0 collective-permute-done.7.there_ref
  80.2 0.4 shard_map.99
  80.6 2.5 %collective-permute-start.8 = (bf16[64,1536]{1,0:T(8,128)(2,1)S(1)}, bf16[64,1536]{1,0:T(8,128)(2,1)S(1)}, u32[]{:S(2)}, u32[]{:S(2)}) collective-permute-start(bf16[64,1536]{1,0:T(8,128)(2,1)S(1)} %get-tuple-element.13), channel_id=1, source_target_pairs={{0,1},{1,0},{2,3},{3,2},{4,5},{5,4},{6,7},{7,6},{8,9},{9,8},{10,11... | collective-permute-start | bytes 589832 | tf_op jit(solution)/shard_map/ppermute | solution.py:244
  83.1 8.2 %all-to-all-done.1.parts_ref = bf16[8,32,1152]{2,1,0:T(8,128)(2,1)S(1)} async-done(((bf16[8,32,1152]{2,1,0:T(8,128)(2,1)}), bf16[8,32,1152]{2,1,0:T(8,128)(2,1)S(1)}, u32[]{:S(2)}, u32[]{:S(2)}) %all-to-all-start.1) | async-done | bytes 589856 | tf_op jit(solution)/shard_map/all_to_all | solution.py:209
  91.3 0.8 shard_map.101
  92.1 19.7 %all-to-all-start.2 = ((bf16[32,2,640]{2,1,0:T(2,128)(2,1)}), bf16[32,2,640]{2,1,0:T(2,128)(2,1)S(1)}, u32[]{:S(2)}, u32[]{:S(2)}) async-start(bf16[32,2,640]{2,1,0:T(2,128)(2,1)} %shard_map.101), calls=%async_computation.2 | async-start | bytes 163840 | tf_op jit(solution)/shard_map/all_to_all | solution.py:227
  111.9 0.0 collective-permute-done.8
  111.9 0.7 fusion
  112.6 26.4 %all-to-all-done.2.parts_ref = bf16[32,2,640]{2,1,0:T(2,128)(2,1)S(1)} async-done(((bf16[32,2,640]{2,1,0:T(2,128)(2,1)}), bf16[32,2,640]{2,1,0:T(2,128)(2,1)S(1)}, u32[]{:S(2)}, u32[]{:S(2)}) %all-to-all-start.2) | async-done | bytes 81952 | tf_op jit(solution)/shard_map/all_to_all | solution.py:227
  139.0 0.7 shard_map.102
  (4 shorter events, 0.1 us)
Async XLA Ops:
  2.9 5.2 %copy-start.3 = (bf16[1,6,1536]{2,1,0:T(8,128)(2,1)S(1)}, bf16[1,6,1536]{2,1,0:T(8,128)(2,1)}, u32[]{:S(2)}) copy-start(bf16[1,6,1536]{2,1,0:T(8,128)(2,1)} %param.11) | copy-start | bytes 55300
  2.9 34.6 %copy-start = (bf16[1,128,1536]{2,1,0:T(8,128)(2,1)S(1)}, bf16[1,128,1536]{2,1,0:T(8,128)(2,1)}, u32[]{:S(2)}) copy-start(bf16[1,128,1536]{2,1,0:T(8,128)(2,1)} %cot_ref.1) | copy-start | bytes 1179652
  2.9 34.5 %copy-start.2 = (f32[4,1536]{1,0:T(4,128)S(1)}, f32[4,1536]{1,0:T(4,128)}, u32[]{:S(2)}) copy-start(f32[4,1536]{1,0:T(4,128)} %table_ref.1) | copy-start | bytes 73732
  2.9 34.6 %copy-start.1 = (bf16[1,128,384]{2,1,0:T(8,128)(2,1)S(1)}, bf16[1,128,384]{2,1,0:T(8,128)(2,1)}, u32[]{:S(2)}) copy-start(bf16[1,128,384]{2,1,0:T(8,128)(2,1)} %q_ref.1) | copy-start | bytes 294916
  2.9 34.6 %all-to-all-start = ((bf16[8,256,384]{2,1,0:T(8,128)(2,1)}), bf16[8,256,384]{2,1,0:T(8,128)(2,1)S(1)}, u32[]{:S(2)}, u32[]{:S(2)}) async-start(bf16[8,256,384]{2,1,0:T(8,128)(2,1)} %shard_map.96), calls=%async_computation | async-start | bytes 3145728 | tf_op jit(solution)/shard_map/all_to_all | solution.py:174
  8.1 3.1 %collective-permute-start = (bf16[6,1536]{1,0:T(8,128)(2,1)S(1)}, bf16[6,1536]{1,0:T(8,128)(2,1)S(1)}, u32[]{:S(2)}, u32[]{:S(2)}) collective-permute-start(bf16[6,1536]{1,0:T(8,128)(2,1)S(1)} %bitcast.4), channel_id=1, source_target_pairs={{0,16},{16,0},{1,17},{17,1},{2,18},{18,2},{3,19},{19,3},{4,20},{20... | collective-permute-start | bytes 55304 | tf_op jit(solution)/shard_map/ppermute | solution.py:176
  11.2 36.1 %collective-permute-start.1 = (bf16[12,1536]{1,0:T(8,128)(2,1)S(1)}, bf16[12,1536]{1,0:T(8,128)(2,1)S(1)}, u32[]{:S(2)}, u32[]{:S(2)}) collective-permute-start(bf16[12,1536]{1,0:T(8,128)(2,1)S(1)} %pad_maximum_fusion.2), channel_id=1, source_target_pairs={{768,0},{802,2},{836,4},{870,6},{904,8},{938,10},{972,12},{1006,14... | collective-permute-start | bytes 110600 | tf_op jit(solution)/shard_map/ppermute | solution.py:179
  26.9 23.1 %collective-permute-start.2 = (bf16[12,1536]{1,0:T(8,128)(2,1)S(1)}, bf16[12,1536]{1,0:T(8,128)(2,1)S(1)}, u32[]{:S(2)}, u32[]{:S(2)}) collective-permute-start(bf16[12,1536]{1,0:T(8,128)(2,1)S(1)} %pad_maximum_fusion.2), channel_id=1, source_target_pairs={{256,0},{290,2},{324,4},{358,6},{392,8},{426,10},{460,12},{494,14}... | collective-permute-start | bytes 110600 | tf_op jit(solution)/shard_map/ppermute | solution.py:178
  40.8 33.5 %collective-permute-start.9 = (bf16[8,32,1152]{2,1,0:T(8,128)(2,1)}, bf16[8,32,1152]{2,1,0:T(8,128)(2,1)S(1)}, u32[]{:S(2)}, u32[]{:S(2)}) collective-permute-start(bf16[8,32,1152]{2,1,0:T(8,128)(2,1)} %get-tuple-element.15), channel_id=1, source_target_pairs={{0,16},{16,0},{1,17},{17,1},{2,18},{18,2},{3,19},{19,3},{4,20},{20... | collective-permute-start | bytes 1769480 | tf_op jit(solution)/shard_map/ppermute | solution.py:198
  50.1 6.2 %collective-permute-start.3 = (bf16[24,1536]{1,0:T(8,128)(2,1)S(1)}, bf16[24,1536]{1,0:T(8,128)(2,1)S(1)}, u32[]{:S(2)}, u32[]{:S(2)}) collective-permute-start(bf16[24,1536]{1,0:T(8,128)(2,1)S(1)} %pad_maximum_fusion.1), channel_id=1, source_target_pairs={{0,8},{8,0},{1,9},{9,1},{2,10},{10,2},{3,11},{11,3},{4,12},{12,4},... | collective-permute-start | bytes 221192 | tf_op jit(solution)/shard_map/ppermute | solution.py:200
  56.4 10.5 %collective-permute-start.4 = (bf16[48,1536]{1,0:T(8,128)(2,1)S(1)}, bf16[48,1536]{1,0:T(8,128)(2,1)S(1)}, u32[]{:S(2)}, u32[]{:S(2)}) collective-permute-start(bf16[48,1536]{1,0:T(8,128)(2,1)S(1)} %pad_maximum_fusion), channel_id=1, source_target_pairs={{0,2},{2,4},{4,6},{6,0},{1,3},{3,5},{5,7},{7,1},{8,10},{10,12},{12... | collective-permute-start | bytes 442376 | tf_op jit(solution)/shard_map/ppermute | solution.py:219
  60.0 10.0 %collective-permute-start.5 = (bf16[48,1536]{1,0:T(8,128)(2,1)S(1)}, bf16[48,1536]{1,0:T(8,128)(2,1)S(1)}, u32[]{:S(2)}, u32[]{:S(2)}) collective-permute-start(bf16[48,1536]{1,0:T(8,128)(2,1)S(1)} %pad_maximum_fusion), channel_id=1, source_target_pairs={{0,4},{2,6},{4,0},{6,2},{1,5},{3,7},{5,1},{7,3},{8,12},{10,14},{12... | collective-permute-start | bytes 442376 | tf_op jit(solution)/shard_map/ppermute | solution.py:219
  63.6 8.3 %collective-permute-start.6 = (bf16[48,1536]{1,0:T(8,128)(2,1)S(1)}, bf16[48,1536]{1,0:T(8,128)(2,1)S(1)}, u32[]{:S(2)}, u32[]{:S(2)}) collective-permute-start(bf16[48,1536]{1,0:T(8,128)(2,1)S(1)} %pad_maximum_fusion), channel_id=1, source_target_pairs={{0,6},{2,0},{4,2},{6,4},{1,7},{3,1},{5,3},{7,5},{8,14},{10,8},{12,... | collective-permute-start | bytes 442376 | tf_op jit(solution)/shard_map/ppermute | solution.py:219
  72.3 7.9 %collective-permute-start.7 = (bf16[192,1536]{1,0:T(8,128)(2,1)S(1)}, bf16[192,1536]{1,0:T(8,128)(2,1)S(1)}, u32[]{:S(2)}, u32[]{:S(2)}) collective-permute-start(bf16[192,1536]{1,0:T(8,128)(2,1)S(1)} %concatenate.17.here_ref), channel_id=1, source_target_pairs={{0,16},{16,0},{1,17},{17,1},{2,18},{18,2},{3,19},{19,3},{4,20},{20... | collective-permute-start | bytes 1769480 | tf_op jit(solution)/shard_map/ppermute | solution.py:236
  75.2 16.2 %all-to-all-start.1 = ((bf16[8,32,1152]{2,1,0:T(8,128)(2,1)}), bf16[8,32,1152]{2,1,0:T(8,128)(2,1)S(1)}, u32[]{:S(2)}, u32[]{:S(2)}) async-start(bf16[8,32,1152]{2,1,0:T(8,128)(2,1)} %shard_map.100), calls=%async_computation.1 | async-start | bytes 1179648 | tf_op jit(solution)/shard_map/all_to_all | solution.py:209
  80.6 31.3 %collective-permute-start.8 = (bf16[64,1536]{1,0:T(8,128)(2,1)S(1)}, bf16[64,1536]{1,0:T(8,128)(2,1)S(1)}, u32[]{:S(2)}, u32[]{:S(2)}) collective-permute-start(bf16[64,1536]{1,0:T(8,128)(2,1)S(1)} %get-tuple-element.13), channel_id=1, source_target_pairs={{0,1},{1,0},{2,3},{3,2},{4,5},{5,4},{6,7},{7,6},{8,9},{9,8},{10,11... | collective-permute-start | bytes 589832 | tf_op jit(solution)/shard_map/ppermute | solution.py:244
  92.1 46.9 %all-to-all-start.2 = ((bf16[32,2,640]{2,1,0:T(2,128)(2,1)}), bf16[32,2,640]{2,1,0:T(2,128)(2,1)S(1)}, u32[]{:S(2)}, u32[]{:S(2)}) async-start(bf16[32,2,640]{2,1,0:T(2,128)(2,1)} %shard_map.101), calls=%async_computation.2 | async-start | bytes 163840 | tf_op jit(solution)/shard_map/all_to_all | solution.py:227

commit v5 on v2

--- a/solution.py
+++ b/solution.py
@@ -18,33 +18,41 @@
 F32 = jnp.float32
 BF16 = jnp.bfloat16
 VM = pl.BlockSpec(memory_space=pltpu.VMEM)
-SM = pl.BlockSpec(memory_space=pltpu.SMEM)
 
 
 def nt_dot(a, b):
     return lax.dot_general(a, b, (((1,), (1,)), ((), ())), preferred_element_type=F32)
 
 
-def scale_kernel(ts_ref, cot_ref, table_ref, scaled_ref, gate_ref):
-    gate = table_ref[pl.ds(ts_ref[0], 1), :]
+def pack_kernel(own_ref, mate_ref, out_ref):
+    rows = jnp.concatenate([own_ref[0].astype(F32), mate_ref[...].astype(F32)], axis=0)
+    tails = [
+        jnp.concatenate([rows[3 * q + s : 3 * q + s + 1, CHUNK:] for s in range(3)], axis=1)
+        for q in range(4)
+    ]
+    out_ref[...] = jnp.concatenate([rows[:, :CHUNK]] + tails, axis=0).astype(BF16)
+
+
+def scale_kernel(ts_ref, si_ref, cot_ref, table_ref, scaled_ref, gate_ref, bias_ref):
+    place = lax.axis_index("yl") * 4 + lax.axis_index("x")
+    spans = lax.broadcasted_iota(jnp.int32, (1, SPANS * TOK), 1) // TOK
+    bias_ref[...] = jnp.where(spans <= jnp.minimum(si_ref[...], place), 0.0, -jnp.inf)
+    step_hit = lax.broadcasted_iota(jnp.int32, (4, 1), 0) == ts_ref[...]
+    gate = jnp.sum(jnp.where(step_hit, table_ref[...], 0.0), axis=0, keepdims=True)
     gate_ref[...] = gate
     scaled_ref[...] = (gate * cot_ref[0].astype(F32)).astype(BF16)
 
 
-def attend_kernel(si_ref, q_ref, kv_ref, scaled_ref, keep_ref, send_ref, att_ref):
-    place = lax.axis_index("yl") * 4 + lax.axis_index("x")
+def attend_kernel(q_ref, kv_ref, scaled_ref, bias_ref, keep_ref, send_ref, att_ref):
     core = lax.axis_index("c")
-    limit = jnp.minimum(place, si_ref[0])
     inv_root = HEAD ** (-0.5)
-    spans = lax.broadcasted_iota(jnp.int32, (1, SPANS * TOK), 1) // TOK
-    visible = spans <= limit
+    bias = bias_ref[...]
     outs = []
     for h in range(HDM // HEAD):
         cols = slice(h * HEAD, (h + 1) * HEAD)
         keys = jnp.concatenate([kv_ref[j, :TOK, cols] for j in range(SPANS)], axis=0)
         values = jnp.concatenate([kv_ref[j, TOK:, cols] for j in range(SPANS)], axis=0)
-        scores = nt_dot(q_ref[0, :, cols], keys) * inv_root
-        scores = jnp.where(visible, scores, -jnp.inf)
+        scores = nt_dot(q_ref[0, :, cols], keys) * inv_root + bias
         weights = jnp.exp(scores - jnp.max(scores, axis=1, keepdims=True))
         probs = (weights / jnp.sum(weights, axis=1, keepdims=True)).astype(BF16)
         outs.append(jnp.dot(probs, values, preferred_element_type=F32).astype(BF16))
@@ -76,16 +84,32 @@
             ref[yl * 4 + 3] = rows[2][:, 384:]
 
 
+def pair_kernel(k_ref, v_ref, out_ref, held, in_sems, sems):
+    loads = [
+        pltpu.make_async_copy(ref.at[0], held.at[i], in_sems.at[i])
+        for i, ref in enumerate((k_ref, v_ref))
+    ]
+    for load in loads:
+        load.start()
+    copies = []
+    for i, load in enumerate(loads):
+        load.wait()
+        for j in range(SPANS):
+            copy = pltpu.make_async_copy(
+                held.at[i], out_ref.at[j, pl.ds(i * TOK, TOK), :], sems.at[i * SPANS + j]
+            )
+            copy.start()
+            copies.append(copy)
+    for copy in copies:
+        copy.wait()
+
+
 def merge_kernel(keep_ref, other_ref, near_ref, far_ref, out_ref):
-    rows = jnp.concatenate([near_ref[...].astype(F32), far_ref[...].astype(F32)], axis=0)
-    tails = [
-        jnp.concatenate([rows[3 * q + s : 3 * q + s + 1, CHUNK:] for s in range(3)], axis=1)
-        for q in range(8)
-    ]
-    block = jnp.concatenate([rows[:, :CHUNK]] + tails, axis=0).astype(BF16)
+    near, far = near_ref[...], far_ref[...]
     for j in range(SPANS):
         out_ref[j, :ZS] = (keep_ref[j] + other_ref[j].astype(F32)).astype(BF16)
-        out_ref[j, ZS:] = block
+        out_ref[j, ZS : ZS + 16] = near
+        out_ref[j, ZS + 16 :] = far
 
 
 def expand_kernel(att_ref, out_ref):
@@ -98,11 +122,11 @@
     for part in range(2):
         side = part ^ core
         for kind in range(4):
-            row = r if kind == 0 else 3 * (r - 24) + kind - 1
-            z = (depth + side * 8 + place - 8 + 16 * (row // 12) + ZS) % ZS
-            t = row % 12
+            row = r % 16
+            t = row if kind == 0 else 3 * (row - 12) + kind - 1
+            z = (depth + side * 8 + place - 8 + 16 * (r // 16) + ZS) % ZS
             feature = (z * 2 + ((t // 6) ^ side)) * 6 + t % 6
-            feature = jnp.where((r < 24) == (kind == 0), feature, -1)
+            feature = jnp.where((row < 12) == (kind == 0), feature, -1)
             pick = (rows == feature).astype(F32).astype(BF16)
             out_ref[part, kind] = jnp.dot(attended, pick, preferred_element_type=F32).astype(BF16)
 
@@ -138,6 +162,13 @@
         here_ref[j] = parts_ref[j, ZS:]
 
 
+def sum_kernel(parts_ref, out_ref):
+    total = jnp.sum(parts_ref[...].astype(F32), axis=0)
+    for j in range(9):
+        row, col = j // 5, (j % 5) * 128
+        out_ref[j] = total[row : row + 1, col : col + 128]
+
+
 def columns(shift):
     pairs = []
     for z in range(ZS):
@@ -155,28 +186,44 @@
 def local(queries, keys, values, proj_weight, gate_table, timestep, span_index, cotangent):
     S = jax.ShapeDtypeStruct
     swap = [(0, 1), (1, 0)]
-    pair = jnp.concatenate([keys[0], values[0]], axis=0)
-    pair = jnp.broadcast_to(pair[None], (SPANS,) + pair.shape)
+    pair = pl.pallas_call(
+        pair_kernel,
+        out_shape=S((SPANS, 2 * TOK, HDM), BF16),
+        in_specs=[pl.BlockSpec(memory_space=pltpu.HBM)] * 2,
+        out_specs=pl.BlockSpec(memory_space=pl.ANY),
+        scratch_shapes=[
+            pltpu.VMEM((2, TOK, HDM), BF16),
+            pltpu.SemaphoreType.DMA((2,)),
+            pltpu.SemaphoreType.DMA((2 * SPANS,)),
+        ],
+        compiler_params=pltpu.CompilerParams(vmem_limit_bytes=67043328),
+    )(keys, values)
     pairs = lax.all_to_all(pair, SEQ, 0, 0, tiled=True)
     every = ("z", "c") + SEQ
     mate = lax.ppermute(proj_weight[0], "c", swap)
-    dozen = jnp.concatenate([proj_weight[0], mate], axis=0)
+    dozen = pl.pallas_call(
+        pack_kernel,
+        out_shape=S((16, CHUNK), BF16),
+        in_specs=[VM, VM],
+        out_specs=VM,
+        compiler_params=vmem(8),
+    )(proj_weight, mate)
     far = lax.ppermute(dozen, every, columns(16))
     near = lax.ppermute(dozen, every, columns(0))
-    scaled, gate = pl.pallas_call(
+    scaled, gate, bias = pl.pallas_call(
         scale_kernel,
-        out_shape=(S((TOK, WIDTH), BF16), S((1, WIDTH), F32)),
-        in_specs=[SM, VM, VM],
-        out_specs=(VM, VM),
-        compiler_params=vmem(8),
-    )(timestep, cotangent, gate_table)
+        out_shape=(S((TOK, WIDTH), BF16), S((1, WIDTH), F32), S((1, SPANS * TOK), F32)),
+        in_specs=[VM, VM, VM, VM],
+        out_specs=(VM, VM, VM),
+        compiler_params=vmem(8),
+    )(timestep.reshape(1, 1), span_index.reshape(1, 1), cotangent, gate_table)
     keep, send, attended = pl.pallas_call(
         attend_kernel,
         out_shape=(S((SPANS, ZS, CHUNK), F32), S((SPANS, ZS, CHUNK), BF16), S((TOK, HDM), BF16)),
-        in_specs=[SM, VM, VM, VM],
+        in_specs=[VM, VM, VM, VM],
         out_specs=(VM, VM, VM),
         compiler_params=vmem(20),
-    )(span_index, queries, pairs, scaled)
+    )(queries, pairs, scaled, bias)
     other = lax.ppermute(send, "c", swap)
     both = pl.pallas_call(
         merge_kernel,
@@ -201,8 +248,13 @@
         compiler_params=vmem(8),
     )(parts)
     last = lax.all_to_all(slices, "z", 0, 0, tiled=True)
-    total = jnp.sum(last.astype(F32), axis=0).reshape(1280)[:CHUNK]
-    weight_grad = total.reshape(1, 9, 128)
+    weight_grad = pl.pallas_call(
+        sum_kernel,
+        out_shape=S((9, 1, 128), F32),
+        in_specs=[VM],
+        out_specs=VM,
+        compiler_params=vmem(8),
+    )(last).reshape(1, 9, 128)
     there = lax.ppermute(here, "c", swap)
     own, away = pl.pallas_call(
         mix_kernel,

time: 146 us -> 144 us (0.986)
  Pallas kernels: 4.49 us -> 7.49 us
  blocking collectives: 28.4 us -> 25.4 us
  local copies, waits for them, and re-layouts: 1.94 us -> 0.03 us
    pallas_call x0 -> x3, Pallas kernels: none -> 2.96 us  [the longest x1 2.26 us: local(): pl.pallas_call(pair_kernel, out_shape=S((SPANS, 2 * TOK, HDM), BF16), in_...]
    all_to_all x1, blocking collectives: 28.4 us -> 25.4 us  [local(): parts = lax.all_to_all(both, SEQ, 0, 0, tiled=True)]
  transfers between devices with their start and end apart: 8 -> 8, of which waited for: 4 -> 4; matrix products, arithmetic and copies ran while one was open for 1% -> 0% of each run, Pallas kernels for 1% -> 1%
where the time goes in v5:
time: 144 us; the launch traced here: 143 us
  starting transfers between devices  72.5 us (50%)
  waiting for transfers between devices  35.1 us (24%)
  blocking collectives  25.4 us (18%)
  Pallas kernels  7.49 us (5%)
  between operations  2.11 us (1%)
    all_to_all x1, blocking collectives, local(): parts = lax.all_to_all(both, SEQ, 0, 0, tiled=True)  25.4 us
    ppermute x1, starting transfers between devices, local(): far = lax.ppermute(dozen, every, columns(16))  24.9 us
    all_to_all x1, waiting for transfers between devices, local(): last = lax.all_to_all(slices, 'z', 0, 0, tiled=True)  20.9 us
    all_to_all x1, starting transfers between devices, local(): last = lax.all_to_all(slices, 'z', 0, 0, tiled=True)  17.8 us
    ppermute x1, starting transfers between devices, local(): other = lax.ppermute(send, 'c', swap)  14.8 us
    all_to_all x1, waiting for transfers between devices, local(): pairs = lax.all_to_all(pair, SEQ, 0, 0, tiled=True)  11.6 us
    all_to_all x1, starting transfers between devices, local(): pairs = lax.all_to_all(pair, SEQ, 0, 0, tiled=True)  5.99 us
    ppermute x1, starting transfers between devices, local(): rest = lax.ppermute(away, 'yh', swap)  4.54 us
  transfers between devices with their start and end apart: 8, of which 4 were waited for; matrix products, arithmetic and copies ran while one was open for 0% of the time, Pallas kernels for 1%

profile of v5, /device:TPU:1, one launch (start us, length us, event | category | flops | bytes accessed | tf_op | source)
XLA Modules:
  0.0 143.4 jit_solution(17509874584397901694)
XLA Ops:
  0.6 2.3 %shard_map.96 = bf16[8,256,384]{2,1,0:T(8,128)(2,1)} custom-call(bf16[1,128,384]{2,1,0:T(8,128)(2,1)} %k_ref.1, bf16[1,128,384]{2,1,0:T(8,128)(2,1)} %v_ref.1), custom_call_target="tpu_custom_call" | custom-call | tf_op jit(solution)/shard_map/pallas_call | solution.py:189
  2.9 0.0 copy-start
  2.9 0.0 copy-start.2
  2.9 0.0 copy-start.1
  2.9 6.0 %all-to-all-start = ((bf16[8,256,384]{2,1,0:T(8,128)(2,1)}), bf16[8,256,384]{2,1,0:T(8,128)(2,1)S(1)}, u32[]{:S(2)}, u32[]{:S(2)}) async-start(bf16[8,256,384]{2,1,0:T(8,128)(2,1)} %shard_map.96), calls=%async_computation | async-start | bytes 3145728 | tf_op jit(solution)/shard_map/all_to_all | solution.py:201
  10.2 0.0 copy-done
  10.2 0.0 copy-done.2
  10.2 0.0 copy-start.3
  10.3 0.2 shard_map.95
  10.5 11.6 %all-to-all-done.kv_ref = bf16[8,256,384]{2,1,0:T(8,128)(2,1)S(1)} async-done(((bf16[8,256,384]{2,1,0:T(8,128)(2,1)}), bf16[8,256,384]{2,1,0:T(8,128)(2,1)S(1)}, u32[]{:S(2)}, u32[]{:S(2)}) %all-to-all-start) | async-done | bytes 1572896 | tf_op jit(solution)/shard_map/all_to_all | solution.py:201
  22.1 0.0 copy-done.1
  22.1 2.4 %shard_map.97 = (f32[8,32,1152]{2,1,0:T(8,128)S(1)}, bf16[8,32,1152]{2,1,0:T(8,128)(2,1)S(1)}, bf16[128,384]{1,0:T(8,128)(2,1)S(1)}) custom-call(bf16[1,128,384]{2,1,0:T(8,128)(2,1)S(1)} %copy-done.1, bf16[8,256,384]{2,1,0:T(8,128)(2,1)S(1)} %all-to-all-done.kv_ref, bf16[128,1536]{1,0:T(8,128)(2,1)S(1)} %get-tuple-element.13.scaled_ref, ...), custom_call_target="tpu_custom_call" | custom-call | tf_op jit(solution)/shard_map/pallas_call | solution.py:220
  24.5 14.8 %collective-permute-start = (bf16[8,32,1152]{2,1,0:T(8,128)(2,1)S(1)}, bf16[8,32,1152]{2,1,0:T(8,128)(2,1)S(1)}, u32[]{:S(2)}, u32[]{:S(2)}) collective-permute-start(bf16[8,32,1152]{2,1,0:T(8,128)(2,1)S(1)} %get-tuple-element.17), channel_id=1, source_target_pairs={{0,16},{16,0},{1,17},{17,1},{2,18},{18,2},{3,19},{19,3},{4,20},{20... | collective-permute-start | bytes 1769480 | tf_op jit(solution)/shard_map/ppermute | solution.py:227
  39.3 0.0 copy-done.3
  39.3 1.9 %collective-permute-start.1 = (bf16[6,1536]{1,0:T(8,128)(2,1)S(1)}, bf16[6,1536]{1,0:T(8,128)(2,1)S(1)}, u32[]{:S(2)}, u32[]{:S(2)}) collective-permute-start(bf16[6,1536]{1,0:T(8,128)(2,1)S(1)} %bitcast.8), channel_id=1, source_target_pairs={{0,16},{16,0},{1,17},{17,1},{2,18},{18,2},{3,19},{19,3},{4,20},{20... | collective-permute-start | bytes 55304 | tf_op jit(solution)/shard_map/ppermute | solution.py:203
  41.3 1.2 collective-permute-done.1.mate_ref
  42.4 0.7 collective-permute-start.2
  43.1 24.9 %collective-permute-start.3 = (bf16[16,1152]{1,0:T(8,128)(2,1)S(1)}, bf16[16,1152]{1,0:T(8,128)(2,1)S(1)}, u32[]{:S(2)}, u32[]{:S(2)}) collective-permute-start(bf16[16,1152]{1,0:T(8,128)(2,1)S(1)} %shard_map.99), channel_id=1, source_target_pairs={{256,0},{290,2},{324,4},{358,6},{392,8},{426,10},{460,12},{494,14}... | collective-permute-start | bytes 110600 | tf_op jit(solution)/shard_map/ppermute | solution.py:211
  68.0 0.0 collective-permute-done.2.near_ref
  68.0 1.4 collective-permute-done.3.far_ref
  69.4 0.0 collective-permute-done.other_ref
  69.4 0.1 shard_map.100
  69.6 25.4 %all_to_all.15.parts_ref = bf16[8,64,1152]{2,1,0:T(8,128)(2,1)S(1)} all-to-all(bf16[8,64,1152]{2,1,0:T(8,128)(2,1)S(1)} %shard_map.100), channel_id=1, replica_groups=mesh['z'=32,'c'=2,'yl'=2,'x'=4,'yh'=2] {'yl','x'}, dimensions={0} | all-to-all | bytes 2359296 | tf_op jit(solution)/shard_map/all_to_all | solution.py:235
  95.0 0.8 shard_map.101
  95.8 1.9 %collective-permute-start.4 = (bf16[8,32,1152]{2,1,0:T(8,128)(2,1)S(1)}, bf16[8,32,1152]{2,1,0:T(8,128)(2,1)S(1)}, u32[]{:S(2)}, u32[]{:S(2)}) collective-permute-start(bf16[8,32,1152]{2,1,0:T(8,128)(2,1)S(1)} %get-tuple-element.18.here_ref), channel_id=1, source_target_pairs={{0,16},{16,0},{1,17},{17,1},{2,18},{18,2},{3,19},{19,3},{4,20},{20... | collective-permute-start | bytes 1769480 | tf_op jit(solution)/shard_map/ppermute | solution.py:258
  97.7 17.8 %all-to-all-start.2 = ((bf16[32,2,640]{2,1,0:T(2,128)(2,1)}), bf16[32,2,640]{2,1,0:T(2,128)(2,1)S(1)}, u32[]{:S(2)}, u32[]{:S(2)}) async-start(bf16[32,2,640]{2,1,0:T(2,128)(2,1)} %get-tuple-element.21), calls=%async_computation.2 | async-start | bytes 163840 | tf_op jit(solution)/shard_map/all_to_all | solution.py:250
  115.5 0.5 shard_map.98.wide_ref
  116.0 0.0 collective-permute-done.4.there_ref
  116.0 0.5 shard_map.102
  116.6 4.5 %collective-permute-start.5 = (bf16[64,1536]{1,0:T(8,128)(2,1)S(1)}, bf16[64,1536]{1,0:T(8,128)(2,1)S(1)}, u32[]{:S(2)}, u32[]{:S(2)}) collective-permute-start(bf16[64,1536]{1,0:T(8,128)(2,1)S(1)} %get-tuple-element.20), channel_id=1, source_target_pairs={{0,1},{1,0},{2,3},{3,2},{4,5},{5,4},{6,7},{7,6},{8,9},{9,8},{10,11... | collective-permute-start | bytes 589832 | tf_op jit(solution)/shard_map/ppermute | solution.py:266
  121.1 20.9 %all-to-all-done.2.parts_ref = bf16[32,2,640]{2,1,0:T(2,128)(2,1)S(1)} async-done(((bf16[32,2,640]{2,1,0:T(2,128)(2,1)}), bf16[32,2,640]{2,1,0:T(2,128)(2,1)S(1)}, u32[]{:S(2)}, u32[]{:S(2)}) %all-to-all-start.2) | async-done | bytes 81952 | tf_op jit(solution)/shard_map/all_to_all | solution.py:250
  142.0 0.7 shard_map.103
  142.7 0.0 collective-permute-done.5
  142.7 0.7 fusion
  (2 shorter events, 0.0 us)
Async XLA Ops:
  2.9 7.3 %copy-start = (bf16[1,128,1536]{2,1,0:T(8,128)(2,1)S(1)}, bf16[1,128,1536]{2,1,0:T(8,128)(2,1)}, u32[]{:S(2)}) copy-start(bf16[1,128,1536]{2,1,0:T(8,128)(2,1)} %cot_ref.1) | copy-start | bytes 1179652
  2.9 7.3 %copy-start.2 = (f32[4,1536]{1,0:T(4,128)S(1)}, f32[4,1536]{1,0:T(4,128)}, u32[]{:S(2)}) copy-start(f32[4,1536]{1,0:T(4,128)} %table_ref.1) | copy-start | bytes 73732
  2.9 19.2 %copy-start.1 = (bf16[1,128,384]{2,1,0:T(8,128)(2,1)S(1)}, bf16[1,128,384]{2,1,0:T(8,128)(2,1)}, u32[]{:S(2)}) copy-start(bf16[1,128,384]{2,1,0:T(8,128)(2,1)} %q_ref.1) | copy-start | bytes 294916
  2.9 19.2 %all-to-all-start = ((bf16[8,256,384]{2,1,0:T(8,128)(2,1)}), bf16[8,256,384]{2,1,0:T(8,128)(2,1)S(1)}, u32[]{:S(2)}, u32[]{:S(2)}) async-start(bf16[8,256,384]{2,1,0:T(8,128)(2,1)} %shard_map.96), calls=%async_computation | async-start | bytes 3145728 | tf_op jit(solution)/shard_map/all_to_all | solution.py:201
  10.2 29.1 %copy-start.3 = (bf16[1,6,1536]{2,1,0:T(8,128)(2,1)S(1)}, bf16[1,6,1536]{2,1,0:T(8,128)(2,1)}, u32[]{:S(2)}) copy-start(bf16[1,6,1536]{2,1,0:T(8,128)(2,1)} %own_ref.1) | copy-start | bytes 55300
  24.5 45.0 %collective-permute-start = (bf16[8,32,1152]{2,1,0:T(8,128)(2,1)S(1)}, bf16[8,32,1152]{2,1,0:T(8,128)(2,1)S(1)}, u32[]{:S(2)}, u32[]{:S(2)}) collective-permute-start(bf16[8,32,1152]{2,1,0:T(8,128)(2,1)S(1)} %get-tuple-element.17), channel_id=1, source_target_pairs={{0,16},{16,0},{1,17},{17,1},{2,18},{18,2},{3,19},{19,3},{4,20},{20... | collective-permute-start | bytes 1769480 | tf_op jit(solution)/shard_map/ppermute | solution.py:227
  39.3 3.1 %collective-permute-start.1 = (bf16[6,1536]{1,0:T(8,128)(2,1)S(1)}, bf16[6,1536]{1,0:T(8,128)(2,1)S(1)}, u32[]{:S(2)}, u32[]{:S(2)}) collective-permute-start(bf16[6,1536]{1,0:T(8,128)(2,1)S(1)} %bitcast.8), channel_id=1, source_target_pairs={{0,16},{16,0},{1,17},{17,1},{2,18},{18,2},{3,19},{19,3},{4,20},{20... | collective-permute-start | bytes 55304 | tf_op jit(solution)/shard_map/ppermute | solution.py:203
  42.4 25.6 %collective-permute-start.2 = (bf16[16,1152]{1,0:T(8,128)(2,1)S(1)}, bf16[16,1152]{1,0:T(8,128)(2,1)S(1)}, u32[]{:S(2)}, u32[]{:S(2)}) collective-permute-start(bf16[16,1152]{1,0:T(8,128)(2,1)S(1)} %shard_map.99), channel_id=1, source_target_pairs={{768,0},{802,2},{836,4},{870,6},{904,8},{938,10},{972,12},{1006,14... | collective-permute-start | bytes 110600 | tf_op jit(solution)/shard_map/ppermute | solution.py:212
  43.1 26.3 %collective-permute-start.3 = (bf16[16,1152]{1,0:T(8,128)(2,1)S(1)}, bf16[16,1152]{1,0:T(8,128)(2,1)S(1)}, u32[]{:S(2)}, u32[]{:S(2)}) collective-permute-start(bf16[16,1152]{1,0:T(8,128)(2,1)S(1)} %shard_map.99), channel_id=1, source_target_pairs={{256,0},{290,2},{324,4},{358,6},{392,8},{426,10},{460,12},{494,14}... | collective-permute-start | bytes 110600 | tf_op jit(solution)/shard_map/ppermute | solution.py:211
  95.8 20.2 %collective-permute-start.4 = (bf16[8,32,1152]{2,1,0:T(8,128)(2,1)S(1)}, bf16[8,32,1152]{2,1,0:T(8,128)(2,1)S(1)}, u32[]{:S(2)}, u32[]{:S(2)}) collective-permute-start(bf16[8,32,1152]{2,1,0:T(8,128)(2,1)S(1)} %get-tuple-element.18.here_ref), channel_id=1, source_target_pairs={{0,16},{16,0},{1,17},{17,1},{2,18},{18,2},{3,19},{19,3},{4,20},{20... | collective-permute-start | bytes 1769480 | tf_op jit(solution)/shard_map/ppermute | solution.py:258
  97.7 44.3 %all-to-all-start.2 = ((bf16[32,2,640]{2,1,0:T(2,128)(2,1)}), bf16[32,2,640]{2,1,0:T(2,128)(2,1)S(1)}, u32[]{:S(2)}, u32[]{:S(2)}) async-start(bf16[32,2,640]{2,1,0:T(2,128)(2,1)} %get-tuple-element.21), calls=%async_computation.2 | async-start | bytes 163840 | tf_op jit(solution)/shard_map/all_to_all | solution.py:250
  116.6 26.1 %collective-permute-start.5 = (bf16[64,1536]{1,0:T(8,128)(2,1)S(1)}, bf16[64,1536]{1,0:T(8,128)(2,1)S(1)}, u32[]{:S(2)}, u32[]{:S(2)}) collective-permute-start(bf16[64,1536]{1,0:T(8,128)(2,1)S(1)} %get-tuple-element.20), channel_id=1, source_target_pairs={{0,1},{1,0},{2,3},{3,2},{4,5},{5,4},{6,7},{7,6},{8,9},{9,8},{10,11... | collective-permute-start | bytes 589832 | tf_op jit(solution)/shard_map/ppermute | solution.py:266

commit v6 on v5

--- a/solution.py
+++ b/solution.py
@@ -54,7 +54,7 @@
         values = jnp.concatenate([kv_ref[j, TOK:, cols] for j in range(SPANS)], axis=0)
         scores = nt_dot(q_ref[0, :, cols], keys) * inv_root + bias
         weights = jnp.exp(scores - jnp.max(scores, axis=1, keepdims=True))
-        probs = (weights / jnp.sum(weights, axis=1, keepdims=True)).astype(BF16)
+        probs = (weights * (1.0 / jnp.sum(weights, axis=1, keepdims=True))).astype(BF16)
         outs.append(jnp.dot(probs, values, preferred_element_type=F32).astype(BF16))
     attended = jnp.concatenate(outs, axis=1)
     att_ref[...] = attended
@@ -104,20 +104,18 @@
         copy.wait()
 
 
-def merge_kernel(keep_ref, other_ref, near_ref, far_ref, out_ref):
-    near, far = near_ref[...], far_ref[...]
-    for j in range(SPANS):
-        out_ref[j, :ZS] = (keep_ref[j] + other_ref[j].astype(F32)).astype(BF16)
-        out_ref[j, ZS : ZS + 16] = near
-        out_ref[j, ZS + 16 :] = far
+def add_kernel(keep_ref, other_ref, out_ref):
+    out_ref[...] = (keep_ref[...] + other_ref[...].astype(F32)).astype(BF16)
 
 
 def expand_kernel(att_ref, out_ref):
     core = lax.axis_index("c")
     depth = lax.axis_index("z")
     attended = att_ref[...]
+    x, yl = lax.axis_index("x"), lax.axis_index("yl")
     p = lax.broadcasted_iota(jnp.int32, (1, 256), 1)
-    place, r = p // 32, p % 32
+    place = (yl ^ ((p // 32) % 2)) * 4 + (x - p // 64 + 4) % 4
+    r = p % 32
     rows = lax.broadcasted_iota(jnp.int32, (HDM, 256), 0)
     for part in range(2):
         side = part ^ core
@@ -136,7 +134,7 @@
     head = jnp.zeros((TOK, CHUNK), F32)
     tail = jnp.zeros((TOK, TAIL), F32)
     for part, ref in ((0, here_ref), (1, there_ref)):
-        block = ref[...].reshape(256, CHUNK)
+        block = ref[...]
         head = head + jnp.dot(wide_ref[part, 0], block, preferred_element_type=F32)
         for s in range(3):
             tail = tail + jnp.dot(
@@ -150,16 +148,21 @@
         send_ref[:, cols] = jnp.where(first, m[64:], m[:64]).astype(BF16)
 
 
-def fold_kernel(parts_ref, out_ref, here_ref):
-    total = parts_ref[0, :ZS].astype(F32)
+def join_kernel(*refs):
+    *parts, out_ref = refs
+    rows = parts[0].shape[0]
+    for i, part in enumerate(parts):
+        out_ref[i * rows : (i + 1) * rows] = part[...]
+
+
+def fold_kernel(parts_ref, out_ref):
+    total = parts_ref[0].astype(F32)
     for j in range(1, SPANS):
-        total = total + parts_ref[j, :ZS].astype(F32)
+        total = total + parts_ref[j].astype(F32)
     total = total.astype(BF16)
     out_ref[:, 0, :] = total[:, :640]
     out_ref[:, 1, :512] = total[:, 640:]
     out_ref[:, 1, 512:] = jnp.zeros((ZS, 128), BF16)
-    for j in range(SPANS):
-        here_ref[j] = parts_ref[j, ZS:]
 
 
 def sum_kernel(parts_ref, out_ref):
@@ -225,13 +228,28 @@
         compiler_params=vmem(20),
     )(queries, pairs, scaled, bias)
     other = lax.ppermute(send, "c", swap)
+    dozens = pl.pallas_call(
+        join_kernel,
+        out_shape=S((32, CHUNK), BF16),
+        in_specs=[VM] * 2,
+        out_specs=VM,
+        compiler_params=vmem(8),
+    )(near, far)
+    beside = lax.ppermute(dozens, "yl", swap)
+    block = pl.pallas_call(
+        join_kernel,
+        out_shape=S((64, CHUNK), BF16),
+        in_specs=[VM] * 2,
+        out_specs=VM,
+        compiler_params=vmem(8),
+    )(dozens, beside)
     both = pl.pallas_call(
-        merge_kernel,
-        out_shape=S((SPANS, 2 * ZS, CHUNK), BF16),
-        in_specs=[VM, VM, VM, VM],
-        out_specs=VM,
-        compiler_params=vmem(8),
-    )(keep, other, near, far)
+        add_kernel,
+        out_shape=S((SPANS, ZS, CHUNK), BF16),
+        in_specs=[VM, VM],
+        out_specs=VM,
+        compiler_params=vmem(8),
+    )(keep, other)
     parts = lax.all_to_all(both, SEQ, 0, 0, tiled=True)
     wide = pl.pallas_call(
         expand_kernel,
@@ -240,11 +258,14 @@
         out_specs=VM,
         compiler_params=vmem(8),
     )(attended)
-    slices, here = pl.pallas_call(
+    blocks = [block]
+    for k in range(1, 4):
+        blocks.append(lax.ppermute(block, "x", [(i, (i + k) % 4) for i in range(4)]))
+    slices = pl.pallas_call(
         fold_kernel,
-        out_shape=(S((ZS, 2, 640), BF16), S((SPANS, ZS, CHUNK), BF16)),
+        out_shape=S((ZS, 2, 640), BF16),
         in_specs=[VM],
-        out_specs=(VM, VM),
+        out_specs=VM,
         compiler_params=vmem(8),
     )(parts)
     last = lax.all_to_all(slices, "z", 0, 0, tiled=True)
@@ -255,6 +276,13 @@
         out_specs=VM,
         compiler_params=vmem(8),
     )(last).reshape(1, 9, 128)
+    here = pl.pallas_call(
+        join_kernel,
+        out_shape=S((256, CHUNK), BF16),
+        in_specs=[VM] * 4,
+        out_specs=VM,
+        compiler_params=vmem(8),
+    )(*blocks)
     there = lax.ppermute(here, "c", swap)
     own, away = pl.pallas_call(
         mix_kernel,

time: 144 us -> 159 us (1.10)
  the two profiles are of different devices: /device:TPU:1 before, /device:TPU:16 now
where the time goes in v6:
time: 159 us; the launch traced here: 158 us
  waiting for transfers between devices  75.8 us (48%)
  starting transfers between devices  71.5 us (45%)
  Pallas kernels  8.31 us (5%)
  between operations  2.16 us (1%)
    all_to_all x1, waiting for transfers between devices, local(): last = lax.all_to_all(slices, 'z', 0, 0, tiled=True)  26.4 us
    all_to_all x1, waiting for transfers between devices, local(): pairs = lax.all_to_all(pair, SEQ, 0, 0, tiled=True)  19.8 us
    all_to_all x1, starting transfers between devices, local(): last = lax.all_to_all(slices, 'z', 0, 0, tiled=True)  17.3 us
    ppermute x1, starting transfers between devices, local(): near = lax.ppermute(dozen, every, columns(0))  15.7 us
    ppermute x1, waiting for transfers between devices, local(): far = lax.ppermute(dozen, every, columns(16))  10.9 us
    ppermute x1, starting transfers between devices, local(): far = lax.ppermute(dozen, every, columns(16))  9.2 us
    ppermute x3, starting transfers between devices, local(): lax.ppermute(block, 'x', [(i, (i + k) % 4) for i in range(4)])  8.97 us
    all_to_all x1, waiting for transfers between devices, local(): parts = lax.all_to_all(both, SEQ, 0, 0, tiled=True)  7.37 us
  transfers between devices with their start and end apart: 13, of which 8 were waited for; matrix products, arithmetic and copies ran while one was open for 0% of the time, Pallas kernels for 2%

profile of v6, /device:TPU:16, one launch (start us, length us, event | category | flops | bytes accessed | tf_op | source)
XLA Modules:
  0.0 158.5 jit_solution(8589223287124805715)
XLA Ops:
  0.6 2.2 %shard_map.96 = bf16[8,256,384]{2,1,0:T(8,128)(2,1)} custom-call(bf16[1,128,384]{2,1,0:T(8,128)(2,1)} %k_ref.1, bf16[1,128,384]{2,1,0:T(8,128)(2,1)} %v_ref.1), custom_call_target="tpu_custom_call" | custom-call | tf_op jit(solution)/shard_map/pallas_call | solution.py:192
  2.9 0.0 copy-start
  2.9 0.0 copy-start.2
  2.9 0.0 copy-start.1
  2.9 5.2 %all-to-all-start = ((bf16[8,256,384]{2,1,0:T(8,128)(2,1)}), bf16[8,256,384]{2,1,0:T(8,128)(2,1)S(1)}, u32[]{:S(2)}, u32[]{:S(2)}) async-start(bf16[8,256,384]{2,1,0:T(8,128)(2,1)} %shard_map.96), calls=%async_computation | async-start | bytes 3145728 | tf_op jit(solution)/shard_map/all_to_all | solution.py:204
  8.1 0.0 copy-start.3
  9.4 0.0 copy-done
  9.4 0.0 copy-done.2
  9.4 0.2 shard_map.95
  9.6 19.8 %all-to-all-done.kv_ref = bf16[8,256,384]{2,1,0:T(8,128)(2,1)S(1)} async-done(((bf16[8,256,384]{2,1,0:T(8,128)(2,1)}), bf16[8,256,384]{2,1,0:T(8,128)(2,1)S(1)}, u32[]{:S(2)}, u32[]{:S(2)}) %all-to-all-start) | async-done | bytes 1572896 | tf_op jit(solution)/shard_map/all_to_all | solution.py:204
  29.4 0.0 copy-done.1
  29.4 2.4 %shard_map.97 = (f32[8,32,1152]{2,1,0:T(8,128)S(1)}, bf16[8,32,1152]{2,1,0:T(8,128)(2,1)S(1)}, bf16[128,384]{1,0:T(8,128)(2,1)S(1)}) custom-call(bf16[1,128,384]{2,1,0:T(8,128)(2,1)S(1)} %copy-done.1, bf16[8,256,384]{2,1,0:T(8,128)(2,1)S(1)} %all-to-all-done.kv_ref, bf16[128,1536]{1,0:T(8,128)(2,1)S(1)} %get-tuple-element.11.scaled_ref, ...), custom_call_target="tpu_custom_call" | custom-call | tf_op jit(solution)/shard_map/pallas_call | solution.py:223
  31.8 1.9 %collective-permute-start.9 = (bf16[8,32,1152]{2,1,0:T(8,128)(2,1)S(1)}, bf16[8,32,1152]{2,1,0:T(8,128)(2,1)S(1)}, u32[]{:S(2)}, u32[]{:S(2)}) collective-permute-start(bf16[8,32,1152]{2,1,0:T(8,128)(2,1)S(1)} %get-tuple-element.17), channel_id=1, source_target_pairs={{0,16},{16,0},{1,17},{17,1},{2,18},{18,2},{3,19},{19,3},{4,20},{20... | collective-permute-start | bytes 1769480 | tf_op jit(solution)/shard_map/ppermute | solution.py:230
  33.7 0.0 copy-done.3
  33.7 2.4 %collective-permute-start = (bf16[6,1536]{1,0:T(8,128)(2,1)S(1)}, bf16[6,1536]{1,0:T(8,128)(2,1)S(1)}, u32[]{:S(2)}, u32[]{:S(2)}) collective-permute-start(bf16[6,1536]{1,0:T(8,128)(2,1)S(1)} %bitcast.8), channel_id=1, source_target_pairs={{0,16},{16,0},{1,17},{17,1},{2,18},{18,2},{3,19},{19,3},{4,20},{20... | collective-permute-start | bytes 55304 | tf_op jit(solution)/shard_map/ppermute | solution.py:206
  36.1 0.8 collective-permute-done.mate_ref
  37.0 15.7 %collective-permute-start.1 = (bf16[16,1152]{1,0:T(8,128)(2,1)S(1)}, bf16[16,1152]{1,0:T(8,128)(2,1)S(1)}, u32[]{:S(2)}, u32[]{:S(2)}) collective-permute-start(bf16[16,1152]{1,0:T(8,128)(2,1)S(1)} %shard_map.99), channel_id=1, source_target_pairs={{768,0},{802,2},{836,4},{870,6},{904,8},{938,10},{972,12},{1006,14... | collective-permute-start | bytes 110600 | tf_op jit(solution)/shard_map/ppermute | solution.py:215
  52.7 9.2 %collective-permute-start.2 = (bf16[16,1152]{1,0:T(8,128)(2,1)S(1)}, bf16[16,1152]{1,0:T(8,128)(2,1)S(1)}, u32[]{:S(2)}, u32[]{:S(2)}) collective-permute-start(bf16[16,1152]{1,0:T(8,128)(2,1)S(1)} %shard_map.99), channel_id=1, source_target_pairs={{256,0},{290,2},{324,4},{358,6},{392,8},{426,10},{460,12},{494,14}... | collective-permute-start | bytes 110600 | tf_op jit(solution)/shard_map/ppermute | solution.py:214
  61.9 0.0 collective-permute-done.1.refs_0_
  61.9 10.9 %collective-permute-done.2.refs_1_ = bf16[16,1152]{1,0:T(8,128)(2,1)S(1)} collective-permute-done((bf16[16,1152]{1,0:T(8,128)(2,1)S(1)}, bf16[16,1152]{1,0:T(8,128)(2,1)S(1)}, u32[]{:S(2)}, u32[]{:S(2)}) %collective-permute-start.2) | collective-permute-done | bytes 36896 | tf_op jit(solution)/shard_map/ppermute | solution.py:214
  72.8 1.9 %collective-permute-start.3 = (bf16[32,1152]{1,0:T(8,128)(2,1)S(1)}, bf16[32,1152]{1,0:T(8,128)(2,1)S(1)}, u32[]{:S(2)}, u32[]{:S(2)}) collective-permute-start(bf16[32,1152]{1,0:T(8,128)(2,1)S(1)} %shard_map.100.refs_0_), channel_id=1, source_target_pairs={{0,8},{8,0},{1,9},{9,1},{2,10},{10,2},{3,11},{11,3},{4,12},{12,4},... | collective-permute-start | bytes 221192 | tf_op jit(solution)/shard_map/ppermute | solution.py:238
  74.7 4.8 %collective-permute-done.3.refs_1_ = bf16[32,1152]{1,0:T(8,128)(2,1)S(1)} collective-permute-done((bf16[32,1152]{1,0:T(8,128)(2,1)S(1)}, bf16[32,1152]{1,0:T(8,128)(2,1)S(1)}, u32[]{:S(2)}, u32[]{:S(2)}) %collective-permute-start.3) | collective-permute-done | bytes 73760 | tf_op jit(solution)/shard_map/ppermute | solution.py:238
  79.6 1.9 %collective-permute-start.4 = (bf16[64,1152]{1,0:T(8,128)(2,1)S(1)}, bf16[64,1152]{1,0:T(8,128)(2,1)S(1)}, u32[]{:S(2)}, u32[]{:S(2)}) collective-permute-start(bf16[64,1152]{1,0:T(8,128)(2,1)S(1)} %shard_map.101.refs_0_), channel_id=1, source_target_pairs={{0,2},{2,4},{4,6},{6,0},{1,3},{3,5},{5,7},{7,1},{8,10},{10,12},{12... | collective-permute-start | bytes 442376 | tf_op jit(solution)/shard_map/ppermute | solution.py:263
  81.5 1.9 %collective-permute-start.5 = (bf16[64,1152]{1,0:T(8,128)(2,1)S(1)}, bf16[64,1152]{1,0:T(8,128)(2,1)S(1)}, u32[]{:S(2)}, u32[]{:S(2)}) collective-permute-start(bf16[64,1152]{1,0:T(8,128)(2,1)S(1)} %shard_map.101.refs_0_), channel_id=1, source_target_pairs={{0,4},{2,6},{4,0},{6,2},{1,5},{3,7},{5,1},{7,3},{8,12},{10,14},{12... | collective-permute-start | bytes 442376 | tf_op jit(solution)/shard_map/ppermute | solution.py:263
  83.4 5.1 %collective-permute-start.6 = (bf16[64,1152]{1,0:T(8,128)(2,1)S(1)}, bf16[64,1152]{1,0:T(8,128)(2,1)S(1)}, u32[]{:S(2)}, u32[]{:S(2)}) collective-permute-start(bf16[64,1152]{1,0:T(8,128)(2,1)S(1)} %shard_map.101.refs_0_), channel_id=1, source_target_pairs={{0,6},{2,0},{4,2},{6,4},{1,7},{3,1},{5,3},{7,5},{8,14},{10,8},{12,... | collective-permute-start | bytes 442376 | tf_op jit(solution)/shard_map/ppermute | solution.py:263
  88.6 2.1 %collective-permute-done.4.refs_1_ = bf16[64,1152]{1,0:T(8,128)(2,1)S(1)} collective-permute-done((bf16[64,1152]{1,0:T(8,128)(2,1)S(1)}, bf16[64,1152]{1,0:T(8,128)(2,1)S(1)}, u32[]{:S(2)}, u32[]{:S(2)}) %collective-permute-start.4) | collective-permute-done | bytes 147488 | tf_op jit(solution)/shard_map/ppermute | solution.py:263
  90.6 0.0 collective-permute-done.5.refs_2_
  90.7 3.6 %collective-permute-done.6.refs_3_ = bf16[64,1152]{1,0:T(8,128)(2,1)S(1)} collective-permute-done((bf16[64,1152]{1,0:T(8,128)(2,1)S(1)}, bf16[64,1152]{1,0:T(8,128)(2,1)S(1)}, u32[]{:S(2)}, u32[]{:S(2)}) %collective-permute-start.6) | collective-permute-done | bytes 147488 | tf_op jit(solution)/shard_map/ppermute | solution.py:263
  94.3 2.4 %collective-permute-start.7 = (bf16[256,1152]{1,0:T(8,128)(2,1)S(1)}, bf16[256,1152]{1,0:T(8,128)(2,1)S(1)}, u32[]{:S(2)}, u32[]{:S(2)}) collective-permute-start(bf16[256,1152]{1,0:T(8,128)(2,1)S(1)} %shard_map.102.here_ref), channel_id=1, source_target_pairs={{0,16},{16,0},{1,17},{17,1},{2,18},{18,2},{3,19},{19,3},{4,20},{20... | collective-permute-start | bytes 1769480 | tf_op jit(solution)/shard_map/ppermute | solution.py:286
  96.7 0.0 collective-permute-done.9.other_ref
  96.7 1.0 shard_map.104
  97.6 3.9 %all-to-all-start.1 = ((bf16[8,32,1152]{2,1,0:T(8,128)(2,1)}), bf16[8,32,1152]{2,1,0:T(8,128)(2,1)S(1)}, u32[]{:S(2)}, u32[]{:S(2)}) async-start(bf16[8,32,1152]{2,1,0:T(8,128)(2,1)} %shard_map.104), calls=%async_computation.1 | async-start | bytes 1179648 | tf_op jit(solution)/shard_map/all_to_all | solution.py:253
  101.6 0.5 shard_map.98.wide_ref
  102.1 0.0 collective-permute-done.7.there_ref
  102.1 0.5 shard_map.103
  102.6 2.6 %collective-permute-start.8 = (bf16[64,1536]{1,0:T(8,128)(2,1)S(1)}, bf16[64,1536]{1,0:T(8,128)(2,1)S(1)}, u32[]{:S(2)}, u32[]{:S(2)}) collective-permute-start(bf16[64,1536]{1,0:T(8,128)(2,1)S(1)} %get-tuple-element.15), channel_id=1, source_target_pairs={{0,1},{1,0},{2,3},{3,2},{4,5},{5,4},{6,7},{7,6},{8,9},{9,8},{10,11... | collective-permute-start | bytes 589832 | tf_op jit(solution)/shard_map/ppermute | solution.py:294
  105.2 7.4 %all-to-all-done.1.parts_ref = bf16[8,32,1152]{2,1,0:T(8,128)(2,1)S(1)} async-done(((bf16[8,32,1152]{2,1,0:T(8,128)(2,1)}), bf16[8,32,1152]{2,1,0:T(8,128)(2,1)S(1)}, u32[]{:S(2)}, u32[]{:S(2)}) %all-to-all-start.1) | async-done | bytes 589856 | tf_op jit(solution)/shard_map/all_to_all | solution.py:253
  112.6 0.8 shard_map.105
  113.3 17.3 %all-to-all-start.2 = ((bf16[32,2,640]{2,1,0:T(2,128)(2,1)}), bf16[32,2,640]{2,1,0:T(2,128)(2,1)S(1)}, u32[]{:S(2)}, u32[]{:S(2)}) async-start(bf16[32,2,640]{2,1,0:T(2,128)(2,1)} %shard_map.105), calls=%async_computation.2 | async-start | bytes 163840 | tf_op jit(solution)/shard_map/all_to_all | solution.py:271
  130.7 0.0 collective-permute-done.8
  130.7 0.7 fusion
  131.4 26.4 %all-to-all-done.2.parts_ref = bf16[32,2,640]{2,1,0:T(2,128)(2,1)S(1)} async-done(((bf16[32,2,640]{2,1,0:T(2,128)(2,1)}), bf16[32,2,640]{2,1,0:T(2,128)(2,1)S(1)}, u32[]{:S(2)}, u32[]{:S(2)}) %all-to-all-start.2) | async-done | bytes 81952 | tf_op jit(solution)/shard_map/all_to_all | solution.py:271
  157.8 0.7 shard_map.106
  (5 shorter events, 0.1 us)
Async XLA Ops:
  2.9 6.5 %copy-start = (bf16[1,128,1536]{2,1,0:T(8,128)(2,1)S(1)}, bf16[1,128,1536]{2,1,0:T(8,128)(2,1)}, u32[]{:S(2)}) copy-start(bf16[1,128,1536]{2,1,0:T(8,128)(2,1)} %cot_ref.1) | copy-start | bytes 1179652
  2.9 6.5 %copy-start.2 = (f32[4,1536]{1,0:T(4,128)S(1)}, f32[4,1536]{1,0:T(4,128)}, u32[]{:S(2)}) copy-start(f32[4,1536]{1,0:T(4,128)} %table_ref.1) | copy-start | bytes 73732
  2.9 26.5 %copy-start.1 = (bf16[1,128,384]{2,1,0:T(8,128)(2,1)S(1)}, bf16[1,128,384]{2,1,0:T(8,128)(2,1)}, u32[]{:S(2)}) copy-start(bf16[1,128,384]{2,1,0:T(8,128)(2,1)} %q_ref.1) | copy-start | bytes 294916
  2.9 26.5 %all-to-all-start = ((bf16[8,256,384]{2,1,0:T(8,128)(2,1)}), bf16[8,256,384]{2,1,0:T(8,128)(2,1)S(1)}, u32[]{:S(2)}, u32[]{:S(2)}) async-start(bf16[8,256,384]{2,1,0:T(8,128)(2,1)} %shard_map.96), calls=%async_computation | async-start | bytes 3145728 | tf_op jit(solution)/shard_map/all_to_all | solution.py:204
  8.1 25.6 %copy-start.3 = (bf16[1,6,1536]{2,1,0:T(8,128)(2,1)S(1)}, bf16[1,6,1536]{2,1,0:T(8,128)(2,1)}, u32[]{:S(2)}) copy-start(bf16[1,6,1536]{2,1,0:T(8,128)(2,1)} %own_ref.1) | copy-start | bytes 55300
  31.8 64.9 %collective-permute-start.9 = (bf16[8,32,1152]{2,1,0:T(8,128)(2,1)S(1)}, bf16[8,32,1152]{2,1,0:T(8,128)(2,1)S(1)}, u32[]{:S(2)}, u32[]{:S(2)}) collective-permute-start(bf16[8,32,1152]{2,1,0:T(8,128)(2,1)S(1)} %get-tuple-element.17), channel_id=1, source_target_pairs={{0,16},{16,0},{1,17},{17,1},{2,18},{18,2},{3,19},{19,3},{4,20},{20... | collective-permute-start | bytes 1769480 | tf_op jit(solution)/shard_map/ppermute | solution.py:230
  33.7 3.2 %collective-permute-start = (bf16[6,1536]{1,0:T(8,128)(2,1)S(1)}, bf16[6,1536]{1,0:T(8,128)(2,1)S(1)}, u32[]{:S(2)}, u32[]{:S(2)}) collective-permute-start(bf16[6,1536]{1,0:T(8,128)(2,1)S(1)} %bitcast.8), channel_id=1, source_target_pairs={{0,16},{16,0},{1,17},{17,1},{2,18},{18,2},{3,19},{19,3},{4,20},{20... | collective-permute-start | bytes 55304 | tf_op jit(solution)/shard_map/ppermute | solution.py:206
  37.0 24.9 %collective-permute-start.1 = (bf16[16,1152]{1,0:T(8,128)(2,1)S(1)}, bf16[16,1152]{1,0:T(8,128)(2,1)S(1)}, u32[]{:S(2)}, u32[]{:S(2)}) collective-permute-start(bf16[16,1152]{1,0:T(8,128)(2,1)S(1)} %shard_map.99), channel_id=1, source_target_pairs={{768,0},{802,2},{836,4},{870,6},{904,8},{938,10},{972,12},{1006,14... | collective-permute-start | bytes 110600 | tf_op jit(solution)/shard_map/ppermute | solution.py:215
  52.7 20.1 %collective-permute-start.2 = (bf16[16,1152]{1,0:T(8,128)(2,1)S(1)}, bf16[16,1152]{1,0:T(8,128)(2,1)S(1)}, u32[]{:S(2)}, u32[]{:S(2)}) collective-permute-start(bf16[16,1152]{1,0:T(8,128)(2,1)S(1)} %shard_map.99), channel_id=1, source_target_pairs={{256,0},{290,2},{324,4},{358,6},{392,8},{426,10},{460,12},{494,14}... | collective-permute-start | bytes 110600 | tf_op jit(solution)/shard_map/ppermute | solution.py:214
  72.8 6.7 %collective-permute-start.3 = (bf16[32,1152]{1,0:T(8,128)(2,1)S(1)}, bf16[32,1152]{1,0:T(8,128)(2,1)S(1)}, u32[]{:S(2)}, u32[]{:S(2)}) collective-permute-start(bf16[32,1152]{1,0:T(8,128)(2,1)S(1)} %shard_map.100.refs_0_), channel_id=1, source_target_pairs={{0,8},{8,0},{1,9},{9,1},{2,10},{10,2},{3,11},{11,3},{4,12},{12,4},... | collective-permute-start | bytes 221192 | tf_op jit(solution)/shard_map/ppermute | solution.py:238
  79.6 11.1 %collective-permute-start.4 = (bf16[64,1152]{1,0:T(8,128)(2,1)S(1)}, bf16[64,1152]{1,0:T(8,128)(2,1)S(1)}, u32[]{:S(2)}, u32[]{:S(2)}) collective-permute-start(bf16[64,1152]{1,0:T(8,128)(2,1)S(1)} %shard_map.101.refs_0_), channel_id=1, source_target_pairs={{0,2},{2,4},{4,6},{6,0},{1,3},{3,5},{5,7},{7,1},{8,10},{10,12},{12... | collective-permute-start | bytes 442376 | tf_op jit(solution)/shard_map/ppermute | solution.py:263
  81.5 9.2 %collective-permute-start.5 = (bf16[64,1152]{1,0:T(8,128)(2,1)S(1)}, bf16[64,1152]{1,0:T(8,128)(2,1)S(1)}, u32[]{:S(2)}, u32[]{:S(2)}) collective-permute-start(bf16[64,1152]{1,0:T(8,128)(2,1)S(1)} %shard_map.101.refs_0_), channel_id=1, source_target_pairs={{0,4},{2,6},{4,0},{6,2},{1,5},{3,7},{5,1},{7,3},{8,12},{10,14},{12... | collective-permute-start | bytes 442376 | tf_op jit(solution)/shard_map/ppermute | solution.py:263
  83.4 10.8 %collective-permute-start.6 = (bf16[64,1152]{1,0:T(8,128)(2,1)S(1)}, bf16[64,1152]{1,0:T(8,128)(2,1)S(1)}, u32[]{:S(2)}, u32[]{:S(2)}) collective-permute-start(bf16[64,1152]{1,0:T(8,128)(2,1)S(1)} %shard_map.101.refs_0_), channel_id=1, source_target_pairs={{0,6},{2,0},{4,2},{6,4},{1,7},{3,1},{5,3},{7,5},{8,14},{10,8},{12,... | collective-permute-start | bytes 442376 | tf_op jit(solution)/shard_map/ppermute | solution.py:263
  94.3 7.8 %collective-permute-start.7 = (bf16[256,1152]{1,0:T(8,128)(2,1)S(1)}, bf16[256,1152]{1,0:T(8,128)(2,1)S(1)}, u32[]{:S(2)}, u32[]{:S(2)}) collective-permute-start(bf16[256,1152]{1,0:T(8,128)(2,1)S(1)} %shard_map.102.here_ref), channel_id=1, source_target_pairs={{0,16},{16,0},{1,17},{17,1},{2,18},{18,2},{3,19},{19,3},{4,20},{20... | collective-permute-start | bytes 1769480 | tf_op jit(solution)/shard_map/ppermute | solution.py:286
  97.6 14.9 %all-to-all-start.1 = ((bf16[8,32,1152]{2,1,0:T(8,128)(2,1)}), bf16[8,32,1152]{2,1,0:T(8,128)(2,1)S(1)}, u32[]{:S(2)}, u32[]{:S(2)}) async-start(bf16[8,32,1152]{2,1,0:T(8,128)(2,1)} %shard_map.104), calls=%async_computation.1 | async-start | bytes 1179648 | tf_op jit(solution)/shard_map/all_to_all | solution.py:253
  102.6 28.0 %collective-permute-start.8 = (bf16[64,1536]{1,0:T(8,128)(2,1)S(1)}, bf16[64,1536]{1,0:T(8,128)(2,1)S(1)}, u32[]{:S(2)}, u32[]{:S(2)}) collective-permute-start(bf16[64,1536]{1,0:T(8,128)(2,1)S(1)} %get-tuple-element.15), channel_id=1, source_target_pairs={{0,1},{1,0},{2,3},{3,2},{4,5},{5,4},{6,7},{7,6},{8,9},{9,8},{10,11... | collective-permute-start | bytes 589832 | tf_op jit(solution)/shard_map/ppermute | solution.py:294
  113.3 44.5 %all-to-all-start.2 = ((bf16[32,2,640]{2,1,0:T(2,128)(2,1)}), bf16[32,2,640]{2,1,0:T(2,128)(2,1)S(1)}, u32[]{:S(2)}, u32[]{:S(2)}) async-start(bf16[32,2,640]{2,1,0:T(2,128)(2,1)} %shard_map.105), calls=%async_computation.2 | async-start | bytes 163840 | tf_op jit(solution)/shard_map/all_to_all | solution.py:271
